TPU v7x, 256 devices: a whole 4x4x8 slice. The times are simulated.
256 devices in a mesh: rows: 64 (over y, z, core), feat: 4 (over x).
Axes of the slice: x: 4, y: 4, z: 8, core: 2. Of those that a mesh axis runs over, the one named last changes fastest.
Arguments:
- gradients: bfloat16 [32768, 128], P('rows'), may hold values from -6 to 6
- hessians: bfloat16 [32768], P('rows'), may hold values from 0.25 to 2
- bin_words: int32 [128, 32768], P('feat', 'rows'), may hold values from 0 to 4095, as said below
- children: int32 [3, 32768], P(None, 'rows'), may hold values from 0 to 1, as said below
- split_feature: int32 [14], replicated, may hold values from 0 to 255
- split_bin: int32 [14], replicated, may hold values from 0 to 62
Outputs:
- split_gain_one: float32 [128, 256], P('rows', 'feat')
- split_gain_two: float32 [256, 256], P('rows', 'feat')
- split_gain_three: float32 [512, 256], P('rows', 'feat')
- child_scores: float32 [3, 64, 2, 128], P(None, 'rows')
Inputs may be any that keep to these rules, and one draw needn't show every extreme that they name: `children`: of the 512 rows of one device, at most 3 / 4, 1 / 2 and 1 / 4 of 512 lie in one node at depths 1, 2 and 3; every device reaches each of these bounds in some node. `bin_words`: word w of panel p, six bits a feature with the lowest bits first, holds the bins of the panel's features 2 w and 2 w + 1, numbered within the panel of 64 features; slots past the panel's last feature are zero. Every bin is below 64.
All inputs are finite; a program needn't handle non-finite values.
Results may differ from a plain program's by a relative error of at most 0.0003.
Values may be sent and summed in bfloat16 or wider, within the bound.
A program may use at most 64 MiB of HBM per device.

v0:
```python
import jax
import jax.numpy as jnp
from jax import lax
from jax.sharding import PartitionSpec as P

FEATURES = 256
BINS = 64
OUT = 128
LEVELS = 3


penalty = 1.0


def as_sent(array):
    return jax.tree.map(lambda a: a.astype(jnp.bfloat16) if a.dtype == jnp.float32 else a, array)


def swapped(block, axis, stride):
    count = lax.axis_size(axis)
    route = []
    for low in range(count):
        high = low | 1 << stride
        if high != low and high < count:
            route += [(low, high), (high, low)]
    return lax.ppermute(block, axis, route)


def unpack_codes(packed):
    shifts = 6 * jnp.arange(2, dtype=jnp.int32)
    pieces = jnp.bitwise_and(jnp.right_shift(packed[:, None, :], shifts[None, :, None]), 63)
    return pieces.reshape(-1, packed.shape[-1])


def split_terms(cumulative, hess_cum):
    total_sum = cumulative[..., -1:, :]
    hess_total = hess_cum[..., -1:]
    right_sum = total_sum - cumulative
    hess_right = hess_total - hess_cum
    split_score = (
        jnp.sum(cumulative * cumulative, -1) / (hess_cum + penalty)
        + jnp.sum(right_sum * right_sum, -1) / (hess_right + penalty)
        - jnp.sum(total_sum * total_sum, -1) / (hess_total + penalty)
    ) / OUT
    return (split_score, right_sum, hess_right)


def front_index(marked, slot_total):
    running = jnp.cumsum(marked.astype(jnp.int32))
    wanted = jnp.arange(slot_total, dtype=jnp.int32) + 1
    source = jnp.searchsorted(running, wanted, side="left")
    filled = wanted <= running[-1]
    return (jnp.minimum(source, marked.shape[0] - 1), filled)


def pick_rows(values, source, filled):
    taken = jnp.take(values, source, axis=0)
    return jnp.where(filled[:, None], taken, jnp.zeros_like(taken))


def pick_slots(values, source, filled):
    taken = jnp.take(values, source, axis=0)
    return jnp.where(filled, taken, jnp.zeros_like(taken))


def pick_columns(values, source, filled):
    taken = jnp.take(values, source, axis=1)
    return jnp.where(filled[None, :], taken, jnp.zeros_like(taken))


def build_hist(bin_codes, grad_rows, hess_rows, block_rows):
    feat_count = bin_codes.shape[0]
    bin_levels = jnp.arange(BINS, dtype=jnp.int32)

    def add_block(step_index, running):
        start_row = step_index * block_rows
        code_block = lax.dynamic_slice_in_dim(bin_codes, start_row, block_rows, 1)
        grad_block = lax.dynamic_slice_in_dim(grad_rows, start_row, block_rows, 0)
        hess_block = lax.dynamic_slice_in_dim(hess_rows, start_row, block_rows, 0)
        one_hot = (code_block[:, None, :] == bin_levels[None, :, None]).astype(jnp.bfloat16)
        one_hot = one_hot.reshape(feat_count * BINS, block_rows)
        return (
            running[0] + jnp.dot(one_hot, grad_block, preferred_element_type=jnp.float32),
            running[1] + jnp.dot(one_hot, hess_block, preferred_element_type=jnp.float32),
        )

    initial = (
        jnp.zeros((feat_count * BINS, OUT), jnp.float32),
        jnp.zeros((feat_count * BINS,), jnp.float32),
    )
    return lax.fori_loop(0, grad_rows.shape[0] // block_rows, add_block, initial)


def on_device(gradients, hessians, bin_words, children, split_feature, split_bin):
    row_count = lax.axis_size("rows")
    top_bit = row_count.bit_length() - 1
    row_index = lax.axis_index("rows")
    panel_index = lax.axis_index("feat")
    feat_dev = FEATURES // lax.axis_size("feat")
    row_dev = gradients.shape[0]
    slot_count = 2 * row_dev
    block_rows = min(256, slot_count)
    pad_rows = slot_count - row_dev
    grad_rows = jnp.concatenate([gradients, jnp.zeros((pad_rows, OUT), jnp.bfloat16)], 0)
    hess_rows = jnp.concatenate([hessians, jnp.zeros((pad_rows,), jnp.bfloat16)], 0)
    word_rows = jnp.concatenate(
        [bin_words, jnp.zeros((bin_words.shape[0], pad_rows), jnp.int32)], 1
    )
    child_rows = jnp.concatenate([children, jnp.zeros((children.shape[0], pad_rows), jnp.int32)], 1)
    splits_total = split_feature.shape[0]
    collected = jnp.zeros((splits_total, 2, OUT), jnp.float32)
    gain_list = []
    slot_list = []
    for level_index in range(LEVELS):
        cross_bit = top_bit - 1 - level_index
        half_bit = jnp.bitwise_and(jnp.right_shift(row_index, cross_bit), 1)
        living = hess_rows > 0
        staying = living & (child_rows[level_index] == half_bit)
        leaving = living & (child_rows[level_index] != half_bit)
        sent_hess = jnp.where(leaving, hess_rows, jnp.zeros_like(hess_rows))
        got_grad, got_hess, got_words, got_child = (
            swapped(grad_rows, "rows", cross_bit),
            swapped(sent_hess, "rows", cross_bit),
            swapped(as_sent(word_rows), "rows", cross_bit).astype(word_rows.dtype),
            swapped(as_sent(child_rows), "rows", cross_bit).astype(child_rows.dtype),
        )
        accepted = jnp.concatenate([staying, got_hess > 0])
        source, filled = front_index(accepted, slot_count)
        grad_rows = pick_rows(jnp.concatenate([grad_rows, got_grad], 0), source, filled)
        hess_rows = pick_slots(jnp.concatenate([hess_rows, got_hess], 0), source, filled)
        word_rows = pick_columns(jnp.concatenate([word_rows, got_words], 1), source, filled)
        child_rows = pick_columns(jnp.concatenate([child_rows, got_child], 1), source, filled)
        bin_codes = unpack_codes(word_rows)
        hist_grad, hist_hess = build_hist(bin_codes, grad_rows, hess_rows, block_rows)
        group_size = row_count >> level_index + 1
        node_count = 2 ** (level_index + 1)
        node_here = jnp.right_shift(row_index, top_bit - level_index - 1)
        share_grad = hist_grad.reshape(feat_dev, BINS * OUT)
        share_hess = hist_hess.reshape(feat_dev, BINS)
        for step_bit in reversed(range(top_bit - level_index - 1)):
            half_rows = share_grad.shape[0] // 2
            upper_half = jnp.bitwise_and(jnp.right_shift(row_index, step_bit), 1) == 1
            keep_grad = jnp.where(upper_half, share_grad[half_rows:], share_grad[:half_rows])
            give_grad = jnp.where(upper_half, share_grad[:half_rows], share_grad[half_rows:])
            keep_hess = jnp.where(upper_half, share_hess[half_rows:], share_hess[:half_rows])
            give_hess = jnp.where(upper_half, share_hess[:half_rows], share_hess[half_rows:])
            got_partial, got_curv = swapped((give_grad, give_hess), "rows", step_bit)
            share_grad = keep_grad + got_partial
            share_hess = keep_hess + got_curv
        share_count = share_grad.shape[0]
        cumulative = jnp.cumsum(share_grad.reshape(share_count, BINS, OUT), axis=1)
        hess_cum = jnp.cumsum(share_hess, axis=1)
        split_score, right_sum, hess_right = split_terms(cumulative, hess_cum)
        gain_list.append(split_score)
        position = jnp.bitwise_and(row_index, group_size - 1)
        split_slot = node_count - 2 + node_here
        feature_id = split_feature[split_slot]
        bin_id = split_bin[split_slot]
        inner_feature = feature_id % feat_dev
        is_owner = (feature_id // feat_dev == panel_index) & (
            inner_feature // share_count == position
        )
        chosen = (
            (jnp.arange(share_count)[:, None] == inner_feature % share_count)
            & (jnp.arange(BINS)[None, :] == bin_id)
            & is_owner
        )
        left_grad = jnp.sum(jnp.where(chosen[..., None], cumulative, 0.0), axis=(0, 1))
        left_hess = jnp.sum(jnp.where(chosen, hess_cum, 0.0))
        right_grad = jnp.sum(jnp.where(chosen[..., None], right_sum, 0.0), axis=(0, 1))
        right_hess = jnp.sum(jnp.where(chosen, hess_right, 0.0))
        child_pair = jnp.stack(
            [
                -left_grad / jnp.sqrt(left_hess + penalty),
                -right_grad / jnp.sqrt(right_hess + penalty),
            ],
            0,
        )
        slot_match = jnp.arange(splits_total) == split_slot
        collected = collected + jnp.where(slot_match[:, None, None], child_pair[None], 0.0)
        slot_list.append(split_slot)
    totals = lax.psum(collected, ("rows", "feat"))
    child_scores = jnp.stack([totals[slot_index] for slot_index in slot_list], 0)[:, None]
    return (gain_list[0], gain_list[1], gain_list[2], child_scores)


def solution(mesh):
    placed = (P("rows", None), P("rows"), P("feat", "rows"), P(None, "rows"), P(), P())
    return jax.shard_map(
        on_device,
        mesh=mesh,
        in_specs=placed,
        out_specs=(
            P("rows", "feat"),
            P("rows", "feat"),
            P("rows", "feat"),
            P(None, "rows", None, None),
        ),
        check_vma=False,
    )
```

profile of v0, /device:TPU:1, one launch (start us, length us, event | category | flops | bytes accessed | tf_op | source)
XLA Modules:
  0.0 707.2 jit_solution(15301522432196689266)
XLA Ops:
  22.0 74.8 %while.98 = (s32[]{:T(128)}, u32[1024]{0:T(1024)S(1)}, u32[1024]{0:T(1024)S(1)}, s32[2048]{0:T(1024)S(1)}, s32[]{:T(128)}, /*index=5*/s32[]{:T(128)}, s32[]{}) while((s32[]{:T(128)}, u32[1024]{0:T(1024)S(1)}, u32[1024]{0:T(1024)S(1)}, s32[2048]{0:T(1024)S(1)}, s32[]{:T(128)}, /*index=5*/s32[]{:T(128)}, s32[]{}) %tuple.223), condition=%wide.region_3.4_spmd.clone, body=%wide.region_2.3_spmd.clone.sunk | while | flops 20484 | bytes 63589 | solution.py:51
  22.0 6.2 gather_fusion
  28.3 6.2 gather_fusion
  34.5 6.2 gather_fusion
  40.7 6.2 gather_fusion
  97.5 6.8 gather_fusion.5
  112.2 74.8 %while.100 = (s32[]{:T(128)}, u32[1024]{0:T(1024)S(1)}, u32[1024]{0:T(1024)S(1)}, s32[2048]{0:T(1024)S(1)}, s32[]{:T(128)}, /*index=5*/s32[]{:T(128)}, s32[]{}) while((s32[]{:T(128)}, u32[1024]{0:T(1024)S(1)}, u32[1024]{0:T(1024)S(1)}, s32[2048]{0:T(1024)S(1)}, s32[]{:T(128)}, /*index=5*/s32[]{:T(128)}, s32[]{}) %tuple.226), condition=%wide.region_14.19_spmd.clone, body=%wide.region_13.18_spmd.clone.sunk | while | flops 20484 | bytes 63589 | solution.py:51
  188.3 6.8 gather_fusion.9
  199.6 7.0 collective-permute-start.26
  210.8 74.8 %while.102 = (s32[]{:T(128)}, u32[1024]{0:T(1024)S(1)}, u32[1024]{0:T(1024)S(1)}, s32[2048]{0:T(1024)S(1)}, s32[]{:T(128)}, /*index=5*/s32[]{:T(128)}, s32[]{}) while((s32[]{:T(128)}, u32[1024]{0:T(1024)S(1)}, u32[1024]{0:T(1024)S(1)}, s32[2048]{0:T(1024)S(1)}, s32[]{:T(128)}, /*index=5*/s32[]{:T(128)}, s32[]{}) %tuple.229), condition=%wide.region_25.30_spmd.clone, body=%wide.region_24.29_spmd.clone.sunk | while | flops 20484 | bytes 63589 | solution.py:51
  286.2 6.8 gather_fusion.13
  326.1 10.0 %collective-permute-done.27 = s32[32,1024]{0,1:T(8,128)} collective-permute-done((s32[32,1024]{0,1:T(8,128)S(1)}, s32[32,1024]{0,1:T(8,128)}, u32[]{:S(2)}, u32[]{:S(2)}) %collective-permute-start.27) | collective-permute-done | bytes 131104 | tf_op jit(solution)/shard_map/ppermute | solution.py:26
  347.9 14.4 %while.99 = (s32[]{:T(128)}, f32[4096,128]{1,0:T(8,128)S(1)}, f32[4096]{0:T(1024)S(1)}, s32[64,1024]{1,0:T(8,128)}, bf16[1024,128]{1,0:T(8,128)(2,1)S(1)}, /*ind...) while((s32[]{:T(128)}, f32[4096,128]{1,0:T(8,128)S(1)}, ...), condition=%wide.region_5.9_spmd.clone, body=%wide.region_4.8_spmd.clone.sunk | while | flops 272637952 | bytes 7735978 | solution.py:91
  371.5 8.5 %collective-permute-start.10 = (f32[8,64]{1,0:T(8,128)S(1)}, f32[8,64]{1,0:T(8,128)S(1)}, u32[]{:S(2)}, u32[]{:S(2)}) collective-permute-start(f32[8,64]{1,0:T(8,128)S(1)} %slice_select_fusion.26), channel_id=1, source_target_pairs={{0,16},{16,0},{4,20},{20,4},{8,24},{24,8},{12,28},{28,12},{32,48},... | collective-permute-start | bytes 6152 | tf_op jit(solution)/shard_map/ppermute | solution.py:26
  395.4 22.7 %while.101 = (s32[]{:T(128)}, f32[4096,128]{1,0:T(8,128)}, f32[4096]{0:T(1024)S(1)}, s32[64,1024]{1,0:T(8,128)}, bf16[1024,128]{1,0:T(8,128)(2,1)S(1)}, /*index=...) while((s32[]{:T(128)}, f32[4096,128]{1,0:T(8,128)}, ...), condition=%wide.region_16.21_spmd.clone, body=%wide.region_15.20_spmd.clone.sunk | while | flops 272637952 | bytes 7735978 | solution.py:91
  420.4 6.4 collective-permute-start.12
  448.5 17.1 %while.103 = (s32[]{:T(128)}, f32[4096,128]{1,0:T(8,128)S(1)}, f32[4096]{0:T(1024)S(1)}, s32[64,1024]{1,0:T(8,128)}, bf16[1024,128]{1,0:T(8,128)(2,1)S(1)}, /*in...) while((s32[]{:T(128)}, f32[4096,128]{1,0:T(8,128)S(1)}, ...), condition=%wide.region_27.32_spmd.clone, body=%wide.region_26.31_spmd.clone.sunk | while | flops 272637952 | bytes 7735978 | solution.py:91
  465.8 7.5 %collective-permute-start.24 = (f32[4,64]{1,0:T(4,128)S(1)}, f32[4,64]{1,0:T(4,128)S(1)}, u32[]{:S(2)}, u32[]{:S(2)}) collective-permute-start(f32[4,64]{1,0:T(4,128)S(1)} %slice_select_fusion.27), channel_id=1, source_target_pairs={{0,4},{4,0},{8,12},{12,8},{16,20},{20,16},{24,28},{28,24},{32,36},... | collective-permute-start | bytes 3080 | tf_op jit(solution)/shard_map/ppermute | solution.py:26
  473.3 18.5 %collective-permute-done.32 = f32[32,64]{1,0:T(8,128)S(1)} collective-permute-done((f32[32,64]{1,0:T(8,128)S(1)}, f32[32,64]{1,0:T(8,128)S(1)}, u32[]{:S(2)}, u32[]{:S(2)}) %collective-permute-start.32) | collective-permute-done | bytes 8224 | tf_op jit(solution)/shard_map/ppermute | solution.py:26
  508.5 73.3 %collective-permute-done.29 = f32[32,8192]{1,0:T(8,128)} collective-permute-done((f32[32,8192]{1,0:T(8,128)}, f32[32,8192]{1,0:T(8,128)}, u32[]{:S(2)}, u32[]{:S(2)}) %collective-permute-start.29) | collective-permute-done | bytes 1048608 | tf_op jit(solution)/shard_map/ppermute | solution.py:26
  585.4 7.6 %collective-permute-done.18 = f32[16,8192]{1,0:T(8,128)S(1)} collective-permute-done((f32[16,8192]{1,0:T(8,128)S(1)}, f32[16,8192]{1,0:T(8,128)S(1)}, u32[]{:S(2)}, u32[]{:S(2)}) %collective-permute-start.18) | collective-permute-done | bytes 524320 | tf_op jit(solution)/shard_map/ppermute | solution.py:26
  593.1 11.2 %collective-permute-done.5 = f32[8,8192]{1,0:T(8,128)S(1)} collective-permute-done((f32[8,8192]{1,0:T(8,128)S(1)}, f32[8,8192]{1,0:T(8,128)S(1)}, u32[]{:S(2)}, u32[]{:S(2)}) %collective-permute-start.5) | collective-permute-done | bytes 262176 | tf_op jit(solution)/shard_map/ppermute | solution.py:26
  606.2 6.3 collective-permute-done.6
  629.4 76.2 %psum.7 = f32[14,2,128]{2,1,0:T(2,128)S(1)} all-reduce(f32[14,2,128]{2,1,0:T(2,128)S(1)} %select_add_fusion.9), channel_id=1, replica_groups=mesh['rows'=64,'feat'=4] {'rows','feat'}, use_global_device_ids=true, to_apply=%region_45.50 | all-reduce | flops 3584 | bytes 28672 | tf_op jit(solution)/shard_map/psum | solution.py:182
  (596 shorter events, 414.0 us)
Async XLA Ops:
  2.1 18.7 %collective-permute-start = (bf16[1024]{0:T(1024)(128)(2,1)S(1)}, bf16[1024]{0:T(1024)(128)(2,1)S(1)}, u32[]{:S(2)}, u32[]{:S(2)}) collective-permute-start(bf16[1024]{0:T(1024)(128)(2,1)S(1)} %and_select_fusion.2), channel_id=1, source_target_pairs={{0,128},{128,0},{4,132},{132,4},{8,136},{136,8},{12,140},{140,12},... | collective-permute-start | bytes 6152 | tf_op jit(solution)/shard_map/ppermute | solution.py:26
  6.6 97.8 %collective-permute-start.13 = (s32[3,1024]{1,0:T(4,128)S(1)}, s32[3,1024]{1,0:T(4,128)S(1)}, u32[]{:S(2)}, u32[]{:S(2)}) collective-permute-start(s32[3,1024]{1,0:T(4,128)S(1)} %concatenate.74), channel_id=1, source_target_pairs={{0,128},{128,0},{4,132},{132,4},{8,136},{136,8},{12,140},{140,12},... | collective-permute-start | bytes 36872 | tf_op jit(solution)/shard_map/ppermute | solution.py:26
  7.4 285.6 %collective-permute-start.1 = (s32[32,1024]{1,0:T(8,128)S(1)}, s32[32,1024]{1,0:T(8,128)S(1)}, u32[]{:S(2)}, u32[]{:S(2)}) collective-permute-start(s32[32,1024]{1,0:T(8,128)S(1)} %concatenate.78), channel_id=1, source_target_pairs={{0,128},{128,0},{4,132},{132,4},{8,136},{136,8},{12,140},{140,12},... | collective-permute-start | bytes 393224 | tf_op jit(solution)/shard_map/ppermute | solution.py:26
  12.1 307.1 %collective-permute-start.2 = (bf16[1024,128]{1,0:T(8,128)(2,1)}, bf16[1024,128]{1,0:T(8,128)(2,1)}, u32[]{:S(2)}, u32[]{:S(2)}) collective-permute-start(bf16[1024,128]{1,0:T(8,128)(2,1)} %concatenate.80), channel_id=1, source_target_pairs={{0,128},{128,0},{4,132},{132,4},{8,136},{136,8},{12,140},{140,12},... | collective-permute-start | bytes 786440 | tf_op jit(solution)/shard_map/ppermute | solution.py:26
  111.1 84.0 %collective-permute-start.25 = (s32[3,1024]{0,1:T(8,128)S(1)}, s32[3,1024]{0,1:T(8,128)S(1)}, u32[]{:S(2)}, u32[]{:S(2)}) collective-permute-start(s32[3,1024]{0,1:T(8,128)S(1)} %bitcast_select_fusion.2), channel_id=1, source_target_pairs={{0,64},{64,0},{4,68},{68,4},{8,72},{72,8},{12,76},{76,12},{16,80},... | collective-permute-start | bytes 36872 | tf_op jit(solution)/shard_map/ppermute | solution.py:26
  199.6 10.6 %collective-permute-start.26 = (bf16[1024]{0:T(1024)(128)(2,1)S(1)}, bf16[1024]{0:T(1024)(128)(2,1)S(1)}, u32[]{:S(2)}, u32[]{:S(2)}) collective-permute-start(bf16[1024]{0:T(1024)(128)(2,1)S(1)} %and_select_fusion), channel_id=1, source_target_pairs={{0,32},{32,0},{4,36},{36,4},{8,40},{40,8},{12,44},{44,12},{16,48},... | collective-permute-start | bytes 6152 | tf_op jit(solution)/shard_map/ppermute | solution.py:26
  298.8 10.4 %collective-permute-start.15 = (s32[32,1024]{0,1:T(8,128)S(1)}, s32[32,1024]{0,1:T(8,128)}, u32[]{:S(2)}, u32[]{:S(2)}) collective-permute-start(s32[32,1024]{0,1:T(8,128)S(1)} %bitcast_select_fusion.3), channel_id=1, source_target_pairs={{0,64},{64,0},{4,68},{68,4},{8,72},{72,8},{12,76},{76,12},{16,80},... | collective-permute-start | bytes 393224 | tf_op jit(solution)/shard_map/ppermute | solution.py:26
  315.7 20.4 %collective-permute-start.27 = (s32[32,1024]{0,1:T(8,128)S(1)}, s32[32,1024]{0,1:T(8,128)}, u32[]{:S(2)}, u32[]{:S(2)}) collective-permute-start(s32[32,1024]{0,1:T(8,128)S(1)} %bitcast_select_fusion.1), channel_id=1, source_target_pairs={{0,32},{32,0},{4,36},{36,4},{8,40},{40,8},{12,44},{44,12},{16,48},... | collective-permute-start | bytes 393224 | tf_op jit(solution)/shard_map/ppermute | solution.py:26
  371.5 9.9 %collective-permute-start.10 = (f32[8,64]{1,0:T(8,128)S(1)}, f32[8,64]{1,0:T(8,128)S(1)}, u32[]{:S(2)}, u32[]{:S(2)}) collective-permute-start(f32[8,64]{1,0:T(8,128)S(1)} %slice_select_fusion.26), channel_id=1, source_target_pairs={{0,16},{16,0},{4,20},{20,4},{8,24},{24,8},{12,28},{28,12},{32,48},... | collective-permute-start | bytes 6152 | tf_op jit(solution)/shard_map/ppermute | solution.py:26
  380.1 10.8 %collective-permute-start.16 = (bf16[1024,128]{1,0:T(8,128)(2,1)S(1)}, bf16[1024,128]{1,0:T(8,128)(2,1)}, u32[]{:S(2)}, u32[]{:S(2)}) collective-permute-start(bf16[1024,128]{1,0:T(8,128)(2,1)S(1)} %get-tuple-element.1187), channel_id=1, source_target_pairs={{0,64},{64,0},{4,68},{68,4},{8,72},{72,8},{12,76},{76,12},{16,80},... | collective-permute-start | bytes 786440 | tf_op jit(solution)/shard_map/ppermute | solution.py:26
  381.4 9.5 %collective-permute-start.11 = (f32[4,64]{1,0:T(4,128)S(1)}, f32[4,64]{1,0:T(4,128)S(1)}, u32[]{:S(2)}, u32[]{:S(2)}) collective-permute-start(f32[4,64]{1,0:T(4,128)S(1)} %slice_select_fusion.28), channel_id=1, source_target_pairs={{0,8},{8,0},{4,12},{12,4},{16,24},{24,16},{20,28},{28,20},{32,40},... | collective-permute-start | bytes 3080 | tf_op jit(solution)/shard_map/ppermute | solution.py:26
  388.4 112.1 %collective-permute-start.3 = (f32[32,8192]{1,0:T(8,128)}, f32[32,8192]{1,0:T(8,128)}, u32[]{:S(2)}, u32[]{:S(2)}) collective-permute-start(f32[32,8192]{1,0:T(8,128)} %select_n.551), channel_id=1, source_target_pairs={{0,64},{64,0},{4,68},{68,4},{8,72},{72,8},{12,76},{76,12},{16,80},... | collective-permute-start | bytes 3145736 | tf_op jit(solution)/shard_map/ppermute | solution.py:26
  418.3 8.5 %collective-permute-start.21 = (f32[32,64]{1,0:T(8,128)S(1)}, f32[32,64]{1,0:T(8,128)S(1)}, u32[]{:S(2)}, u32[]{:S(2)}) collective-permute-start(f32[32,64]{1,0:T(8,128)S(1)} %select_n.603), channel_id=1, source_target_pairs={{0,32},{32,0},{4,36},{36,4},{8,40},{40,8},{12,44},{44,12},{16,48},... | collective-permute-start | bytes 24584 | tf_op jit(solution)/shard_map/ppermute | solution.py:26
  427.8 16.1 %collective-permute-start.28 = (bf16[1024,128]{1,0:T(8,128)(2,1)S(1)}, bf16[1024,128]{1,0:T(8,128)(2,1)}, u32[]{:S(2)}, u32[]{:S(2)}) collective-permute-start(bf16[1024,128]{1,0:T(8,128)(2,1)S(1)} %get-tuple-element.1189), channel_id=1, source_target_pairs={{0,32},{32,0},{4,36},{36,4},{8,40},{40,8},{12,44},{44,12},{16,48},... | collective-permute-start | bytes 786440 | tf_op jit(solution)/shard_map/ppermute | solution.py:26
  431.3 12.6 %collective-permute-start.23 = (f32[8,64]{1,0:T(8,128)S(1)}, f32[8,64]{1,0:T(8,128)S(1)}, u32[]{:S(2)}, u32[]{:S(2)}) collective-permute-start(f32[8,64]{1,0:T(8,128)S(1)} %slice_select_fusion.25), channel_id=1, source_target_pairs={{0,8},{8,0},{4,12},{12,4},{16,24},{24,16},{20,28},{28,20},{32,40},... | collective-permute-start | bytes 6152 | tf_op jit(solution)/shard_map/ppermute | solution.py:26
  437.8 67.4 %collective-permute-start.17 = (f32[32,8192]{1,0:T(8,128)}, f32[32,8192]{1,0:T(8,128)}, u32[]{:S(2)}, u32[]{:S(2)}) collective-permute-start(f32[32,8192]{1,0:T(8,128)} %select_n.589), channel_id=1, source_target_pairs={{0,32},{32,0},{4,36},{36,4},{8,40},{40,8},{12,44},{44,12},{16,48},... | collective-permute-start | bytes 3145736 | tf_op jit(solution)/shard_map/ppermute | solution.py:26
  465.7 26.1 %collective-permute-start.32 = (f32[32,64]{1,0:T(8,128)S(1)}, f32[32,64]{1,0:T(8,128)S(1)}, u32[]{:S(2)}, u32[]{:S(2)}) collective-permute-start(f32[32,64]{1,0:T(8,128)S(1)} %select_n.632), channel_id=1, source_target_pairs={{0,16},{16,0},{4,20},{20,4},{8,24},{24,8},{12,28},{28,12},{32,48},... | collective-permute-start | bytes 24584 | tf_op jit(solution)/shard_map/ppermute | solution.py:26
  465.8 26.2 %collective-permute-start.24 = (f32[4,64]{1,0:T(4,128)S(1)}, f32[4,64]{1,0:T(4,128)S(1)}, u32[]{:S(2)}, u32[]{:S(2)}) collective-permute-start(f32[4,64]{1,0:T(4,128)S(1)} %slice_select_fusion.27), channel_id=1, source_target_pairs={{0,4},{4,0},{8,12},{12,8},{16,20},{20,16},{24,28},{28,24},{32,36},... | collective-permute-start | bytes 3080 | tf_op jit(solution)/shard_map/ppermute | solution.py:26
  499.6 82.2 %collective-permute-start.29 = (f32[32,8192]{1,0:T(8,128)}, f32[32,8192]{1,0:T(8,128)}, u32[]{:S(2)}, u32[]{:S(2)}) collective-permute-start(f32[32,8192]{1,0:T(8,128)} %select_n.621), channel_id=1, source_target_pairs={{0,16},{16,0},{4,20},{20,4},{8,24},{24,8},{12,28},{28,12},{32,48},... | collective-permute-start | bytes 3145736 | tf_op jit(solution)/shard_map/ppermute | solution.py:26
  502.0 81.4 %collective-permute-start.4 = (f32[16,8192]{1,0:T(8,128)S(1)}, f32[16,8192]{1,0:T(8,128)S(1)}, u32[]{:S(2)}, u32[]{:S(2)}) collective-permute-start(f32[16,8192]{1,0:T(8,128)S(1)} %slice_select_fusion.9), channel_id=1, source_target_pairs={{0,32},{32,0},{4,36},{36,4},{8,40},{40,8},{12,44},{44,12},{16,48},... | collective-permute-start | bytes 1572872 | tf_op jit(solution)/shard_map/ppermute | solution.py:26
  506.6 86.3 %collective-permute-start.18 = (f32[16,8192]{1,0:T(8,128)S(1)}, f32[16,8192]{1,0:T(8,128)S(1)}, u32[]{:S(2)}, u32[]{:S(2)}) collective-permute-start(f32[16,8192]{1,0:T(8,128)S(1)} %slice_select_fusion.8), channel_id=1, source_target_pairs={{0,16},{16,0},{4,20},{20,4},{8,24},{24,8},{12,28},{28,12},{32,48},... | collective-permute-start | bytes 1572872 | tf_op jit(solution)/shard_map/ppermute | solution.py:26
  583.2 35.7 %collective-permute-start.30 = (f32[16,8192]{1,0:T(8,128)S(1)}, f32[16,8192]{1,0:T(8,128)S(1)}, u32[]{:S(2)}, u32[]{:S(2)}) collective-permute-start(f32[16,8192]{1,0:T(8,128)S(1)} %slice_select_fusion.7), channel_id=1, source_target_pairs={{0,8},{8,0},{4,12},{12,4},{16,24},{24,16},{20,28},{28,20},{32,40},... | collective-permute-start | bytes 1572872 | tf_op jit(solution)/shard_map/ppermute | solution.py:26
  583.4 20.8 %collective-permute-start.5 = (f32[8,8192]{1,0:T(8,128)S(1)}, f32[8,8192]{1,0:T(8,128)S(1)}, u32[]{:S(2)}, u32[]{:S(2)}) collective-permute-start(f32[8,8192]{1,0:T(8,128)S(1)} %slice_select_fusion.12), channel_id=1, source_target_pairs={{0,16},{16,0},{4,20},{20,4},{8,24},{24,8},{12,28},{28,12},{32,48},... | collective-permute-start | bytes 786440 | tf_op jit(solution)/shard_map/ppermute | solution.py:26
  604.7 13.5 %collective-permute-start.19 = (f32[8,8192]{1,0:T(8,128)S(1)}, f32[8,8192]{1,0:T(8,128)S(1)}, u32[]{:S(2)}, u32[]{:S(2)}) collective-permute-start(f32[8,8192]{1,0:T(8,128)S(1)} %slice_select_fusion.11), channel_id=1, source_target_pairs={{0,8},{8,0},{4,12},{12,4},{16,24},{24,16},{20,28},{28,20},{32,40},... | collective-permute-start | bytes 786440 | tf_op jit(solution)/shard_map/ppermute | solution.py:26
  (32 other events, 304.2 us)
where the time goes:
time: 718 us; the launch traced here: 707 us
  local copies, waits for them, and re-layouts  310 us (43%)
  waiting for transfers between devices  147 us (20%)
  blocking collectives  76.2 us (11%)
  starting transfers between devices  69.7 us (10%)
  other arithmetic  58 us (8%)
  matrix products  30.3 us (4%)
  between operations  13.5 us (2%)
    gather x36, local copies, waits for them, and re-layouts, front_index(): source = jnp.searchsorted(running, wanted, side='left')  222 us
    ppermute x35, waiting for transfers between devices, swapped(): return lax.ppermute(block, axis, route)  147 us
    psum x1, blocking collectives, on_device(): totals = lax.psum(collected, ('rows', 'feat'))  76.2 us
    ppermute x35, starting transfers between devices, swapped(): return lax.ppermute(block, axis, route)  69.7 us
    dot_general x12, matrix products, add_block(): jnp.dot(one_hot, grad_block, preferred_element_type=jnp.float32)  22.6 us
    gather x3, local copies, waits for them, and re-layouts, pick_slots(): taken = jnp.take(values, source, axis=0)  20.4 us
    gather x5, local copies, waits for them, and re-layouts, pick_columns(): taken = jnp.take(values, source, axis=1)  19 us
  transfers between devices with their start and end apart: 35, of which 14 were waited for; matrix products, arithmetic and copies ran while one was open for 52% of the time, Pallas kernels for 0%

commit v1 on v0

v1 whole, which is shorter than its diff:
```python
import jax
import jax.numpy as jnp
from jax import lax
from jax.experimental import pallas as pl
from jax.experimental.pallas import tpu as pltpu
from jax.sharding import PartitionSpec as P

BINS = 64
OUT = 128
SPLITS = 14
ROW_DEV = 512
SLOTS = 128
NY, NZ, NX = 4, 8, 4
HEAD = 144
ROWS_ALL = HEAD + 64
ROWS_DST = HEAD + 16
KEEP = 136
MESH = pl.DeviceIdType.MESH
F32 = jnp.float32
BF16 = jnp.bfloat16

penalty = 1.0
ZZ_ORDER = (0, 3, 1, 2)


def gray(two_bits):
    return two_bits + (two_bits // 2) * (5 - 2 * two_bits)


def block_of(y, parity):
    block = 2 * (((y + 1) // 2) % 2) + y // 2
    return block + parity * (3 - 2 * block)


def nt_dot(left, right):
    return lax.dot_general(left, right, (((1,), (1,)), ((), ())), preferred_element_type=F32)


def gains_of(left):
    total = jnp.broadcast_to(left[:, 127:128], left.shape)
    right = total - left

    def term(part):
        square = part[:OUT] * part[:OUT]
        return jnp.sum(square, axis=0, keepdims=True) / (part[OUT:OUT + 1] + penalty)

    return (term(left) + term(right) - term(total)) / OUT


def kernel(
    split_feature, split_bin, grad_ref, hess_ref, word_ref, child_ref,
    one_ref, two_ref, three_ref, child_out,
    feed, sent, got_z, got_y, acc, half, deep, sib, mid, low,
    gain3, home3, gain2, home2, part, part_y, mine_z, part_z, mine_x, part_x,
    z_send, z_recv, y_send, y_recv, core_send, core_recv, sib_send, sib_recv,
    low_send, low_recv, g3_send, g3_recv, g2_send, g2_recv,
    py_send, py_recv, pz_send, pz_recv, px_send, px_recv,
):
    row = lax.axis_index("rows")
    x = lax.axis_index("feat")
    core = row % 2
    z = (row // 2) % NZ
    y = row // 16
    parity = z % 2
    order = gray(z // 2)
    node = 4 * parity + order
    bit0 = order % 2
    bit1 = order // 2
    block = block_of(y, parity)

    def at(y_to, z_to, core_to):
        return y_to * 16 + z_to * 2 + core_to

    def remote(src, dst, send, recv, row_to, x_to=None):
        return pltpu.make_async_remote_copy(
            src_ref=src, dst_ref=dst, send_sem=send, recv_sem=recv,
            device_id=(row_to, x if x_to is None else x_to), device_id_type=MESH,
        )

    def arrived(ref, sem):
        pltpu.make_async_copy(ref, ref, sem).wait()

    barrier = pltpu.get_barrier_semaphore()

    def greet(row_to, x_to):
        pl.semaphore_signal(barrier, inc=1, device_id=(row_to, x_to), device_id_type=MESH)

    for step in range(1, NZ):
        greet(at(y, (z + step) % NZ, core), x)
    for step in range(1, NY):
        greet(at((y + step) % NY, z, core), x)
    for step in range(1, 2 * NX):
        greet(at(y, z, (core + step) % 2), (x + step // 2) % NX)

    child = child_ref[...]
    node1 = child[0:1]
    node2 = node1 * 2 + child[1:2]
    node3 = node2 * 2 + child[2:3]
    at_node = (lax.broadcasted_iota(jnp.int32, (8, ROW_DEV), 0) == node3).astype(F32)
    upto = (
        lax.broadcasted_iota(jnp.int32, (ROW_DEV, ROW_DEV), 0)
        <= lax.broadcasted_iota(jnp.int32, (ROW_DEV, ROW_DEV), 1)
    ).astype(F32).astype(BF16)
    running = jnp.dot(at_node.astype(BF16), upto, preferred_element_type=F32)
    rank = jnp.sum(at_node * running, axis=0, keepdims=True).astype(jnp.int32) - 1
    low_bits = jnp.bitwise_and(node3, 3)
    node_z = 2 * jnp.bitwise_xor(low_bits, jnp.right_shift(low_bits, 1)) + jnp.right_shift(node3, 2)
    slot = node_z * SLOTS + rank

    hess = hess_ref[...].astype(F32)
    feed[0:OUT, :] = grad_ref[...].astype(F32).T.astype(BF16)
    feed[OUT:HEAD, :] = jnp.concatenate(
        [hess, jnp.zeros((HEAD - OUT - 1, ROW_DEV), F32)], 0
    ).astype(BF16)
    words = word_ref[...]
    natural = jnp.concatenate(
        [jnp.bitwise_and(words, 63), jnp.bitwise_and(jnp.right_shift(words, 6), 63)], 0
    ).astype(F32).astype(BF16)
    spot64 = lax.broadcasted_iota(jnp.int32, (64, 1), 0)
    source64 = (
        32 * jnp.bitwise_and(jnp.right_shift(spot64, 3), 1)
        + 16 * jnp.right_shift(spot64, 5)
        + 2 * jnp.bitwise_and(spot64, 7)
        + jnp.bitwise_and(jnp.right_shift(spot64, 4), 1)
    )
    moved = (lax.broadcasted_iota(jnp.int32, (64, 64), 1) == source64).astype(F32).astype(BF16)
    feed[HEAD:ROWS_ALL, :] = jnp.dot(moved, natural, preferred_element_type=F32).astype(BF16)

    packed = feed[...]
    pl.semaphore_wait(barrier, (NZ - 1) + (NY - 1) + (2 * NX - 1))
    for pair in range(NZ // 2):
        wanted = lax.broadcasted_iota(jnp.int32, (2 * SLOTS, ROW_DEV), 0) + pair * 2 * SLOTS
        pick = (wanted == slot).astype(F32).astype(BF16)
        chosen = nt_dot(packed, pick).astype(BF16)
        for side in range(2):
            z_to = 2 * pair + side
            sent[z_to] = chosen[:, side * SLOTS:(side + 1) * SLOTS]

            @pl.when(z_to != z)
            def _(z_to=z_to):
                remote(
                    sent.at[z_to], got_z.at[z], z_send.at[z_to], z_recv.at[z], at(y, z_to, core)
                ).start()

            @pl.when(z_to == z)
            def _(z_to=z_to):
                pltpu.make_async_copy(sent.at[z_to], got_z.at[z], z_recv.at[z]).start()

    rows32 = lax.broadcasted_iota(jnp.int32, (32, 1), 0)
    yy = jnp.right_shift(rows32, 3)
    which = jnp.bitwise_and(jnp.right_shift(rows32, 1), 3)
    right_side = jnp.bitwise_and(rows32, 1)
    is_one, is_two = which == 0, which == 1
    node_row = jnp.where(
        is_one, jnp.right_shift(yy, 1), jnp.where(is_two, yy, 2 * yy + which - 2)
    )
    split_row = node_row + jnp.where(is_one, 0, jnp.where(is_two, 2, 6))
    feature_row = jnp.zeros((32, 1), jnp.int32)
    bin_row = jnp.zeros((32, 1), jnp.int32)
    for s in range(SPLITS):
        feature_row = jnp.where(split_row == s, split_feature[s], feature_row)
        bin_row = jnp.where(split_row == s, split_bin[s], bin_row)
    inner = jnp.bitwise_and(feature_row, 63)
    place = (
        32 * jnp.right_shift(inner, 5)
        + 16 * jnp.bitwise_and(jnp.right_shift(inner, 1), 1)
        + 8 * jnp.bitwise_and(inner, 1)
        + jnp.bitwise_and(jnp.right_shift(inner, 2), 7)
    )
    panel_row = jnp.right_shift(feature_row, 6)
    spot = (lax.broadcasted_iota(jnp.int32, (32, 64), 1) == place).astype(F32).astype(BF16)
    code_row = jnp.dot(spot, feed[HEAD:ROWS_ALL, :], preferred_element_type=F32).astype(jnp.int32)
    node_here = jnp.where(is_one, node1, jnp.where(is_two, node2, node3))
    goes_right = (code_row > bin_row).astype(jnp.int32)
    wanted_row = (node_here == node_row) & (panel_row == x) & (goes_right == right_side)
    wanted_row = wanted_row.astype(F32)
    sums = jnp.dot(wanted_row.astype(BF16), grad_ref[...], preferred_element_type=F32)
    sums_h = jnp.sum(wanted_row * hess, axis=1, keepdims=True)
    for y_to in range(NY):
        part[y_to, 0:8] = sums[8 * y_to:8 * y_to + 8]
        part[y_to, 8:16] = jnp.broadcast_to(sums_h[8 * y_to:8 * y_to + 8], (8, OUT))
    acc[...] = jnp.zeros_like(acc)
    for step in range(1, NY):
        y_to = (y + step) % NY
        remote(
            part.at[y_to], part_y.at[y], py_send.at[step], py_recv.at[y], at(y_to, z, core)
        ).start()
    pltpu.make_async_copy(part.at[y], part_y.at[y], py_recv.at[y]).start()

    for step in (0, 1, 7, 2, 6, 3, 5, 4):
        z_from = (z + step) % NZ
        arrived(got_z.at[z_from], z_recv.at[z_from])
        for y_step in (1, 3, 2):
            y_to = (y + y_step) % NY
            start = pl.multiple_of(HEAD + 16 * block_of(y_to, parity), 16)
            remote(
                got_z.at[z_from, pl.ds(0, HEAD)], got_y.at[y, z_from, pl.ds(0, HEAD)],
                y_send.at[y_step], y_recv.at[y], at(y_to, z, core),
            ).start()
            remote(
                got_z.at[z_from, pl.ds(start, 16)], got_y.at[y, z_from, pl.ds(HEAD, 16)],
                y_send.at[y_step], y_recv.at[y], at(y_to, z, core),
            ).start()
        start = pl.multiple_of(HEAD + 16 * block, 16)
        pltpu.make_async_copy(
            got_z.at[z_from, pl.ds(0, HEAD)], got_y.at[y, z_from, pl.ds(0, HEAD)], y_recv.at[y]
        ).start()
        pltpu.make_async_copy(
            got_z.at[z_from, pl.ds(start, 16)], got_y.at[y, z_from, pl.ds(HEAD, 16)], y_recv.at[y]
        ).start()

    for y_from in range(NY):
        arrived(part_y.at[y_from], py_recv.at[y_from])
    mine_z[...] = (part_y[0] + part_y[1]) + (part_y[2] + part_y[3])

    bins = lax.broadcasted_iota(jnp.int32, (BINS, 1), 0).astype(F32)

    def add_rows(step, carry):
        y_from = (y + gray(step)) % NY
        arrived(got_y.at[y_from], y_recv.at[y_from])
        values = jnp.concatenate([got_y[y_from, i, 0:HEAD, :] for i in range(NZ)], 1)
        codes = jnp.concatenate(
            [got_y[y_from, i, HEAD:ROWS_DST, :] for i in range(NZ)], 1
        ).astype(F32)
        for pair in range(4):
            masks = []
            for place_index in (2 * (pair % 2), 2 * (pair % 2) + 1):
                zh = 2 * ZZ_ORDER[place_index] + pair // 2
                for i in (zh, 8 + zh):
                    masks.append((codes[i:i + 1] <= bins).astype(F32).astype(BF16))
            found = nt_dot(values, jnp.concatenate(masks, 0))
            acc[2 * pair] += found[:KEEP, 0:128]
            acc[2 * pair + 1] += found[:KEEP, 128:256]
        return carry

    lax.fori_loop(0, NY, add_rows, 0)

    own = 2 * bit0
    other = 2 * (1 - bit0)
    buddy = at(y, z, 1 - core)
    for turn, first_place in ((0, other), (1, own)):
        remote(
            acc.at[pl.ds(4 * (1 - core) + first_place, 2)], half.at[pl.ds(first_place, 2)],
            core_send.at[turn], core_recv.at[turn], buddy,
        ).start()

    for step in range(1, NZ):
        remote(
            mine_z, part_z.at[z], pz_send.at[step], pz_recv.at[z], at(y, (z + step) % NZ, core)
        ).start()
    pltpu.make_async_copy(mine_z, part_z.at[z], pz_recv.at[z]).start()

    arrived(half.at[pl.ds(other, 2)], core_recv.at[0])
    for i in range(2):
        deep[other + i] = acc[4 * core + other + i] + half[other + i]
    sibling = at(y, 2 * gray(2 * bit1 + 1 - bit0) + parity, core)
    to_sibling = remote(deep.at[pl.ds(other, 2)], sib, sib_send, sib_recv, sibling)
    to_sibling.start()
    arrived(half.at[pl.ds(own, 2)], core_recv.at[1])
    for i in range(2):
        deep[own + i] = acc[4 * core + own + i] + half[own + i]
    for i in range(4):
        gain3[i] = gains_of(deep[i])
    spot3 = 2 * core + block % 2
    for i in range(4):
        row_to = 8 * node + 4 * (block // 2) + ZZ_ORDER[i]

        @pl.when(row_to != row)
        def _(i=i, row_to=row_to):
            remote(gain3.at[i], home3.at[spot3], g3_send.at[i], g3_recv.at[spot3], row_to).start()

        @pl.when(row_to == row)
        def _(i=i):
            pltpu.make_async_copy(gain3.at[i], home3.at[spot3], g3_recv.at[spot3]).start()

    for z_from in range(NZ):
        arrived(part_z.at[z_from], pz_recv.at[z_from])
    total_z = part_z[0]
    for z_from in range(1, NZ):
        total_z = total_z + part_z[z_from]
    mine_x[...] = total_z
    here = 2 * x + core
    for step in range(1, 2 * NX):
        remote(
            mine_x, part_x.at[here], px_send.at[step], px_recv.at[here],
            at(y, z, (core + step) % 2), (x + step // 2) % NX,
        ).start()
    pltpu.make_async_copy(mine_x, part_x.at[here], px_recv.at[here]).start()

    arrived(sib, sib_recv)
    places = (bit0, 3 - bit0)
    homes1 = []
    for i in range(2):
        mid[i] = deep[own + i] + sib[i]
        row_to = at(2 * parity + block // 2, 2 * places[i] + core, block % 2)
        homes1.append(row_to)

        @pl.when(row_to != row)
        def _(i=i, row_to=row_to):
            remote(mid.at[i], low.at[bit1], low_send.at[i], low_recv.at[bit1], row_to).start()

        @pl.when(row_to == row)
        def _(i=i):
            pltpu.make_async_copy(mid.at[i], low.at[bit1], low_recv.at[bit1]).start()

    homes2 = []
    spot2 = block % 2
    for i in range(2):
        gain2[i] = gains_of(mid[i])
        row_to = 16 * (node // 2) + 8 * (block // 2) + 2 * places[i] + core
        homes2.append(row_to)

        @pl.when(row_to != row)
        def _(i=i, row_to=row_to):
            remote(gain2.at[i], home2.at[spot2], g2_send.at[i], g2_recv.at[spot2], row_to).start()

        @pl.when(row_to == row)
        def _(i=i):
            pltpu.make_async_copy(gain2.at[i], home2.at[spot2], g2_recv.at[spot2]).start()

    for i in range(4):
        arrived(home3.at[i], g3_recv.at[i])
        three_ref[2 * i:2 * i + 1, :] = home3[i, :, 0:64]
        three_ref[2 * i + 1:2 * i + 2, :] = home3[i, :, 64:128]

    for i in range(2 * NX):
        arrived(part_x.at[i], px_recv.at[i])
    total_x = part_x[0]
    for i in range(1, 2 * NX):
        total_x = total_x + part_x[i]
    scores = -total_x[0:8] / jnp.sqrt(total_x[8:16] + penalty)
    child_out[0, 0] = scores[0:2]
    child_out[1, 0] = scores[2:4]
    child_out[2, 0] = jnp.where(z < NZ // 2, scores[4:6], scores[6:8])

    for i in range(2):
        arrived(low.at[i], low_recv.at[i])
    last = gains_of(low[0] + low[1])
    one_ref[0:1, :] = last[:, 0:64]
    one_ref[1:2, :] = last[:, 64:128]
    for i in range(2):
        arrived(home2.at[i], g2_recv.at[i])
        two_ref[2 * i:2 * i + 1, :] = home2[i, :, 0:64]
        two_ref[2 * i + 1:2 * i + 2, :] = home2[i, :, 64:128]

    for z_to in range(NZ):
        @pl.when(z_to != z)
        def _(z_to=z_to):
            arrived(sent.at[z_to], z_send.at[z_to])
    for step in range(1, NY):
        arrived(part.at[step], py_send.at[step])
        arrived(got_y.at[step], y_send.at[step])
    for turn in range(2):
        arrived(half.at[pl.ds(0, 2)], core_send.at[turn])
    for step in range(1, NZ):
        arrived(mine_z, pz_send.at[step])
    for step in range(1, 2 * NX):
        arrived(mine_x, px_send.at[step])
    to_sibling.wait_send()
    for i in range(4):
        @pl.when(8 * node + 4 * (block // 2) + ZZ_ORDER[i] != row)
        def _(i=i):
            arrived(gain3.at[i], g3_send.at[i])
    for i in range(2):
        @pl.when(homes1[i] != row)
        def _(i=i):
            arrived(mid.at[i], low_send.at[i])

        @pl.when(homes2[i] != row)
        def _(i=i):
            arrived(gain2.at[i], g2_send.at[i])


def on_device(gradients, hessians, bin_words, children, split_feature, split_bin):
    dma = pltpu.SemaphoreType.DMA
    vmem = pl.BlockSpec(memory_space=pltpu.VMEM)
    smem = pl.BlockSpec(memory_space=pltpu.SMEM)
    return pl.pallas_call(
        kernel,
        out_shape=(
            jax.ShapeDtypeStruct((2, BINS), F32),
            jax.ShapeDtypeStruct((4, BINS), F32),
            jax.ShapeDtypeStruct((8, BINS), F32),
            jax.ShapeDtypeStruct((3, 1, 2, OUT), F32),
        ),
        in_specs=[smem, smem, vmem, vmem, vmem, vmem],
        out_specs=(vmem,) * 4,
        scratch_shapes=[
            pltpu.VMEM((ROWS_ALL, ROW_DEV), BF16),
            pltpu.VMEM((NZ, ROWS_ALL, SLOTS), BF16),
            pltpu.VMEM((NZ, ROWS_ALL, SLOTS), BF16),
            pltpu.VMEM((NY, NZ, ROWS_DST, SLOTS), BF16),
            pltpu.VMEM((8, KEEP, 128), F32),
            pltpu.VMEM((4, KEEP, 128), F32),
            pltpu.VMEM((4, KEEP, 128), F32),
            pltpu.VMEM((2, KEEP, 128), F32),
            pltpu.VMEM((2, KEEP, 128), F32),
            pltpu.VMEM((2, KEEP, 128), F32),
            pltpu.VMEM((4, 1, 128), F32),
            pltpu.VMEM((4, 1, 128), F32),
            pltpu.VMEM((2, 1, 128), F32),
            pltpu.VMEM((2, 1, 128), F32),
            pltpu.VMEM((NY, 16, 128), F32),
            pltpu.VMEM((NY, 16, 128), F32),
            pltpu.VMEM((16, 128), F32),
            pltpu.VMEM((NZ, 16, 128), F32),
            pltpu.VMEM((16, 128), F32),
            pltpu.VMEM((2 * NX, 16, 128), F32),
            dma((NZ,)), dma((NZ,)), dma((NY,)), dma((NY,)), dma((2,)), dma((2,)), dma, dma,
            dma((2,)), dma((2,)), dma((4,)), dma((4,)), dma((2,)), dma((2,)),
            dma((NY,)), dma((NY,)), dma((NZ,)), dma((NZ,)), dma((2 * NX,)), dma((2 * NX,)),
        ],
        compiler_params=pltpu.CompilerParams(
            collective_id=0, has_side_effects=True, vmem_limit_bytes=32 << 20
        ),
    )(split_feature, split_bin, gradients, hessians.reshape(1, -1), bin_words, children)


def solution(mesh):
    placed = (P("rows", None), P("rows"), P("feat", "rows"), P(None, "rows"), P(), P())
    return jax.shard_map(
        on_device,
        mesh=mesh,
        in_specs=placed,
        out_specs=(
            P("rows", "feat"),
            P("rows", "feat"),
            P("rows", "feat"),
            P(None, "rows", None, None),
        ),
        check_vma=False,
    )
```

time: 718 us -> 57.4 us (0.08); the launches traced: 707 us -> 56.9 us
  local copies, waits for them, and re-layouts: 310 us -> 5.45 us
  waiting for transfers between devices: 147 us -> 0 us
  blocking collectives: 76.2 us -> 0 us
  starting transfers between devices: 69.7 us -> 0 us
  other arithmetic: 58 us -> 0 us
  Pallas kernels: 0 us -> 50.8 us
  matrix products: 30.3 us -> 0 us
  between operations: 13.5 us -> 0.67 us
    gather x47 -> x0, local copies, waits for them, and re-layouts: 272 us -> none  [the longest x36 222 us: front_index(): source = jnp.searchsorted(running, wanted, side='left')]
    ppermute x35 -> x0, waiting for transfers between devices: 147 us -> none  [swapped(): return lax.ppermute(block, axis, route)]
    psum x1 -> x0, blocking collectives: 76.2 us -> none  [on_device(): totals = lax.psum(collected, ('rows', 'feat'))]
    ppermute x35 -> x0, starting transfers between devices: 69.7 us -> none  [swapped(): return lax.ppermute(block, axis, route)]
    pallas_call x0 -> x1, Pallas kernels: none -> 50.8 us  [on_device(): pl.pallas_call(kernel, out_shape=(jax.ShapeDtypeStruct((2, BINS), F32), j...]
    dot_general x24 -> x0, matrix products: 30.3 us -> none  [the longest x12 22.6 us: add_block(): jnp.dot(one_hot, grad_block, preferred_element_type=jnp.float32)]
    eq x23 -> x0, other arithmetic: 16.7 us -> none  [the longest x12 8.55 us: add_block(): code_block[:, None, :] == bin_levels[None, :, None]]
    dynamic_slice x38 -> x0, local copies, waits for them, and re-layouts: 15.5 us -> none  [the longest x12 10.3 us: add_block(): code_block = lax.dynamic_slice_in_dim(bin_codes, start_row, block_rows, 1)]
  transfers between devices with their start and end apart: 35 -> 0, of which waited for: 14 -> 0; matrix products, arithmetic and copies ran while one was open for 52% -> 0% of each run, Pallas kernels for 0% -> 0%
where the time goes in v1:
time: 57.4 us; the launch traced here: 56.9 us
  Pallas kernels  50.8 us (89%)
  local copies, waits for them, and re-layouts  5.45 us (9%)
  between operations  0.67 us (1%)
    pallas_call x1, Pallas kernels, on_device(): pl.pallas_call(kernel, out_shape=(jax.ShapeDtypeStruct((2, BINS), F32), j...  50.8 us
    unnamed x14, local copies, waits for them, and re-layouts  4.75 us

profile of v1, /device:TPU:1, one launch (start us, length us, event | category | flops | bytes accessed | tf_op | source)
XLA Modules:
  0.0 56.9 jit_solution(17745685247534411909)
XLA Ops:
  0.6 0.0 copy-start.4
  0.6 0.0 copy-start.3
  0.7 0.7 %reshape.11.hess_ref = bf16[1,512]{1,0:T(2,128)(2,1)S(1)} reshape(bf16[512]{0:T(512)(128)(2,1)} %param.7) | data formatting | bytes 2048 | tf_op jit(solution)/shard_map/reshape | solution.py:416
  1.3 0.0 copy-done.4
  1.3 0.0 copy-done.3
  1.4 0.0 copy-start
  1.4 0.9 %copy-done = bf16[512,128]{1,0:T(8,128)(2,1)S(1)} copy-done((bf16[512,128]{1,0:T(8,128)(2,1)S(1)}, bf16[512,128]{1,0:T(8,128)(2,1)}, u32[]{:S(2)}) %copy-start) | copy-done | bytes 131096
  2.3 0.0 copy-start.1
  2.3 0.8 %copy-done.1 = s32[32,512]{1,0:T(8,128)S(1)} copy-done((s32[32,512]{1,0:T(8,128)S(1)}, s32[32,512]{1,0:T(8,128)}, u32[]{:S(2)}) %copy-start.1) | copy-done | bytes 65560
  3.1 0.0 copy-start.2
  3.1 0.7 %copy-done.2 = s32[3,512]{1,0:T(4,128)S(1)} copy-done((s32[3,512]{1,0:T(4,128)S(1)}, s32[3,512]{1,0:T(4,128)}, u32[]{:S(2)}) %copy-start.2) | copy-done | bytes 6168
  3.8 50.8 %shard_map.93 = (f32[2,64]{1,0:T(2,128)S(1)}, f32[4,64]{1,0:T(4,128)S(1)}, f32[8,64]{1,0:T(8,128)S(1)}, f32[3,1,2,128]{3,2,1,0:T(2,128)S(1)}) custom-call(s32[14]{0:T(128)S(1)} %copy-done.3, s32[14]{0:T(128)S(1)} %copy-done.4, bf16[512,128]{1,0:T(8,128)(2,1)S(1)} %copy-done, bf16[1,512]{1,0:T(2,128)(2,1)S(1)} %reshape.11.hess_ref, s32[32,512]{1,0:T(8,128)S(1)} %copy-done.1, ...), custom_call_target="tpu_custom_call" | custom-call | tf_op jit(solution)/shard_map/pallas_call | solution.py:378
  54.6 0.6 copy.14
  55.2 0.6 %copy.15 = f32[4,64]{1,0:T(4,128)} copy(f32[4,64]{1,0:T(4,128)S(1)} %get-tuple-element.9) | data formatting | bytes 2048
  55.7 0.6 %copy.16 = f32[8,64]{1,0:T(8,128)} copy(f32[8,64]{1,0:T(8,128)S(1)} %get-tuple-element.10) | data formatting | bytes 4096
  56.3 0.6 %copy.17 = f32[3,1,2,128]{3,2,1,0:T(2,128)} copy(f32[3,1,2,128]{3,2,1,0:T(2,128)S(1)} %get-tuple-element.11) | data formatting | bytes 6144
Async XLA Ops:
  0.6 0.7 %copy-start.4 = (s32[14]{0:T(128)S(1)}, s32[14]{0:T(128)}, u32[]{:S(2)}) copy-start(s32[14]{0:T(128)} %split_bin.1) | copy-start | bytes 172
  0.6 0.7 %copy-start.3 = (s32[14]{0:T(128)S(1)}, s32[14]{0:T(128)}, u32[]{:S(2)}) copy-start(s32[14]{0:T(128)} %split_feature.1) | copy-start | bytes 172
  1.4 0.9 %copy-start = (bf16[512,128]{1,0:T(8,128)(2,1)S(1)}, bf16[512,128]{1,0:T(8,128)(2,1)}, u32[]{:S(2)}) copy-start(bf16[512,128]{1,0:T(8,128)(2,1)} %grad_ref.1) | copy-start | bytes 393220
  2.3 0.8 %copy-start.1 = (s32[32,512]{1,0:T(8,128)S(1)}, s32[32,512]{1,0:T(8,128)}, u32[]{:S(2)}) copy-start(s32[32,512]{1,0:T(8,128)} %word_ref.1) | copy-start | bytes 196612
  3.1 0.7 %copy-start.2 = (s32[3,512]{1,0:T(4,128)S(1)}, s32[3,512]{1,0:T(4,128)}, u32[]{:S(2)}) copy-start(s32[3,512]{1,0:T(4,128)} %child_ref.1) | copy-start | bytes 18436

commit v2 on v1

v2 whole, which is shorter than its diff:
```python
import jax
import jax.numpy as jnp
from jax import lax
from jax.experimental import pallas as pl
from jax.experimental.pallas import tpu as pltpu
from jax.sharding import PartitionSpec as P

BINS = 64
OUT = 128
LEVELS = 3
SPLITS = 14
ROW_DEV = 512
SLOTS = 128
NY, NZ, NX = 4, 8, 4
HALF = OUT // 2
PIECE = HALF + 64
GOES_Y = HALF + 16
KEEP = OUT + 8
MESH = pl.DeviceIdType.MESH
F32 = jnp.float32
BF16 = jnp.bfloat16

penalty = 1.0
NEAR = (0, 1, 7, 2, 6, 3, 5, 4)


def block_of(y, upper):
    block = 2 * (((y + 1) // 2) % 2) + y // 2
    return block + upper * (3 - 2 * block)


def nt_dot(left, right):
    return lax.dot_general(left, right, (((1,), (1,)), ((), ())), preferred_element_type=F32)


def ones_where(condition):
    return condition.astype(F32).astype(BF16)


def gains_of(left):
    total = jnp.broadcast_to(left[:, 127:128], left.shape)
    right = total - left

    def term(part):
        square = part[:OUT] * part[:OUT]
        return jnp.sum(square, axis=0, keepdims=True) / (part[OUT:OUT + 1] + penalty)

    return (term(left) + term(right) - term(total)) / OUT


def kernel(
    split_feature_any, split_bin_any, grad_any, hess_any, word_any, child_any,
    one_ref, two_ref, three_ref, child_out,
    split_feature, split_bin, grad_ref, hess_ref, word_ref, child_ref,
    sent, sent_h, got_z, got_h, got_y, got_yh, got_x, codes_here,
    acc, half, deep, sib, mid, low,
    gain3, home3, gain2, home2, part, part_y, mine_z, part_z, mine_x, part_x,
    in_sem, z_send, z_recv, zh_send, zh_recv, y_send, y_recv, yh_send, yh_recv,
    relay_send, x_send, x_recv, core_send, core_recv, sib_send, sib_recv,
    low_send, low_recv, g3_send, g3_recv, g2_send, g2_recv,
    py_send, py_recv, pz_send, pz_recv, px_send, px_recv,
):
    row = lax.axis_index("rows")
    x = lax.axis_index("feat")
    core = row % 2
    z = (row // 2) % NZ
    y = row // 16
    upper = z // 4
    block = block_of(y, upper)
    kind = (z + upper) % 2
    own = 2 * kind
    other = 2 - own
    leaving = []

    def at(y_to, z_to, core_to):
        return y_to * 16 + z_to * 2 + core_to

    def remote(src, dst, send, recv, row_to, x_to=None):
        return pltpu.make_async_remote_copy(
            src_ref=src, dst_ref=dst, send_sem=send, recv_sem=recv,
            device_id=(row_to, x if x_to is None else x_to), device_id_type=MESH,
        )

    def arrived(ref, sem):
        pltpu.make_async_copy(ref, ref, sem).wait()

    def left_with(ref, sem):
        leaving.append(lambda: arrived(ref, sem))

    inputs = [
        pltpu.make_async_copy(src, dst, in_sem.at[i])
        for i, (src, dst) in enumerate((
            (child_any, child_ref), (hess_any, hess_ref), (word_any, word_ref),
            (grad_any, grad_ref), (split_feature_any, split_feature), (split_bin_any, split_bin),
        ))
    ]
    for copy in inputs:
        copy.start()

    barrier = pltpu.get_barrier_semaphore()

    def greet(row_to, x_to):
        pl.semaphore_signal(barrier, inc=1, device_id=(row_to, x_to), device_id_type=MESH)

    for step in (4, 3, 5, 2, 6, 1, 7):
        greet(at(y, (z + step) % NZ, core), x)
    for step in (2, 1, 3):
        greet(at((y + step) % NY, z, core), x)
    for step in range(1, 2 * NX):
        greet(at(y, z, (core + step) % 2), (x + step // 2) % NX)
    for copy in inputs:
        copy.wait()

    child = child_ref[...]
    node1 = child[0:1]
    node2 = node1 * 2 + child[1:2]
    node3 = node2 * 2 + child[2:3]
    at_node = (lax.broadcasted_iota(jnp.int32, (8, ROW_DEV), 0) == node3).astype(F32)
    upto = ones_where(
        lax.broadcasted_iota(jnp.int32, (ROW_DEV, ROW_DEV), 0)
        <= lax.broadcasted_iota(jnp.int32, (ROW_DEV, ROW_DEV), 1)
    )
    running = jnp.dot(at_node.astype(BF16), upto, preferred_element_type=F32)
    rank = jnp.sum(at_node * running, axis=0, keepdims=True).astype(jnp.int32) - 1
    slot = node3 * SLOTS + rank

    hess = hess_ref[...].reshape(1, ROW_DEV).astype(F32)
    outputs_all = grad_ref[...].astype(F32).T
    outputs_half = jnp.where(x % 2 == 0, outputs_all[:HALF], outputs_all[HALF:]).astype(BF16)
    words = word_ref[...]
    natural = jnp.concatenate(
        [jnp.bitwise_and(words, 63), jnp.bitwise_and(jnp.right_shift(words, 6), 63)], 0
    ).astype(F32).astype(BF16)
    spot64 = lax.broadcasted_iota(jnp.int32, (64, 1), 0)
    source64 = (
        32 * jnp.bitwise_and(jnp.right_shift(spot64, 3), 1)
        + 16 * jnp.right_shift(spot64, 5)
        + 2 * jnp.bitwise_and(spot64, 7)
        + jnp.bitwise_and(jnp.right_shift(spot64, 4), 1)
    )
    moved = ones_where(lax.broadcasted_iota(jnp.int32, (64, 64), 1) == source64)
    code_rows = jnp.dot(moved, natural, preferred_element_type=F32).astype(BF16)
    hess_tile = jnp.concatenate([hess, jnp.zeros((15, ROW_DEV), F32)], 0).astype(BF16)
    packed = jnp.concatenate([outputs_half, code_rows, hess_tile], 0)
    for pair in range(NZ // 2):
        wanted = lax.broadcasted_iota(jnp.int32, (2 * SLOTS, ROW_DEV), 0) + pair * 2 * SLOTS
        chosen = nt_dot(packed, ones_where(wanted == slot))
        for side in range(2):
            lanes = slice(side * SLOTS, (side + 1) * SLOTS)
            sent[2 * pair + side] = chosen[:PIECE, lanes].astype(BF16)
            sent_h[2 * pair + side] = chosen[PIECE:PIECE + 1, lanes]
    got_h[0] = sent_h[z]

    pl.semaphore_wait(barrier, (NZ - 1) + (NY - 1) + (2 * NX - 1))
    for step in (1, 7, 2, 6, 3, 5, 4):
        z_to = (z + step) % NZ
        place = NEAR.index((NZ - step) % NZ)
        remote(
            sent.at[z_to], got_z.at[place - 1], z_send.at[step], z_recv.at[place], at(y, z_to, core)
        ).start()
        left_with(sent.at[step], z_send.at[step])
    for step in (1, 7, 2, 6, 3, 5, 4):
        z_to = (z + step) % NZ
        place = NEAR.index((NZ - step) % NZ)
        remote(
            sent_h.at[z_to], got_h.at[place], zh_send, zh_recv, at(y, z_to, core)
        ).start()
    left_with(got_h.at[pl.ds(1, NZ - 1)], zh_send)

    rows32 = lax.broadcasted_iota(jnp.int32, (32, 1), 0)
    yy = jnp.right_shift(rows32, 3)
    which = jnp.bitwise_and(jnp.right_shift(rows32, 1), 3)
    right_side = jnp.bitwise_and(rows32, 1)
    is_one, is_two = which == 0, which == 1
    node_row = jnp.where(
        is_one, jnp.right_shift(yy, 1), jnp.where(is_two, yy, 2 * yy + which - 2)
    )
    split_row = node_row + jnp.where(is_one, 0, jnp.where(is_two, 2, 6))
    feature_row = jnp.zeros((32, 1), jnp.int32)
    bin_row = jnp.zeros((32, 1), jnp.int32)
    for s in range(SPLITS):
        feature_row = jnp.where(split_row == s, split_feature[s], feature_row)
        bin_row = jnp.where(split_row == s, split_bin[s], bin_row)
    inner = jnp.bitwise_and(feature_row, 63)
    place = (
        32 * jnp.right_shift(inner, 5)
        + 16 * jnp.bitwise_and(jnp.right_shift(inner, 1), 1)
        + 8 * jnp.bitwise_and(inner, 1)
        + jnp.bitwise_and(jnp.right_shift(inner, 2), 7)
    )
    panel_row = jnp.right_shift(feature_row, 6)
    spot = ones_where(lax.broadcasted_iota(jnp.int32, (32, 64), 1) == place)
    code_row = jnp.dot(spot, code_rows, preferred_element_type=F32).astype(jnp.int32)
    node_here = jnp.where(is_one, node1, jnp.where(is_two, node2, node3))
    goes_right = (code_row > bin_row).astype(jnp.int32)
    wanted_row = (node_here == node_row) & (panel_row == x) & (goes_right == right_side)
    wanted_row = wanted_row.astype(F32)
    sums = jnp.dot(wanted_row.astype(BF16), grad_ref[...], preferred_element_type=F32)
    sums_h = jnp.sum(wanted_row * hess, axis=1, keepdims=True)
    for y_to in range(NY):
        part[y_to, 0:8] = sums[8 * y_to:8 * y_to + 8]
        part[y_to, 8:16] = jnp.broadcast_to(sums_h[8 * y_to:8 * y_to + 8], (8, OUT))
    for step in range(1, NY):
        y_to = (y + step) % NY
        remote(
            part.at[y_to], part_y.at[y], py_send.at[step], py_recv.at[y], at(y_to, z, core)
        ).start()
        left_with(part.at[step], py_send.at[step])
    pltpu.make_async_copy(part.at[y], part_y.at[y], py_recv.at[y]).start()

    def piece(place):
        return sent.at[z] if place == 0 else got_z.at[place - 1]

    def to_x(src, offset, place):
        step = 1 - 2 * (place % 2)
        remote(
            src, got_x.at[offset, place], x_send.at[place % 2], x_recv.at[offset],
            row, (x + step) % NX,
        ).start()

    def from_z(group):
        for place in (2 * group, 2 * group + 1):
            if place:
                arrived(got_z.at[place - 1], z_recv.at[place])
            here = piece(place)
            for step in (1, 3):
                remote(
                    here.at[pl.ds(0, HALF)], got_y.at[NY - step - 1, place, pl.ds(0, HALF)],
                    y_send.at[step], y_recv.at[NY - step - 1, group], at((y + step) % NY, z, core),
                ).start()
            for step in (1, 3, 2):
                y_to = (y + step) % NY
                start = pl.multiple_of(HALF + 16 * block_of(y_to, upper), 16)
                remote(
                    here.at[pl.ds(start, 16)], got_y.at[NY - step - 1, place, pl.ds(HALF, 16)],
                    y_send.at[step], y_recv.at[NY - step - 1, group], at(y_to, z, core),
                ).start()
            to_x(here.at[pl.ds(0, HALF)], 0, place)

    def from_y(offset, group):
        arrived(got_y.at[offset - 1, pl.ds(2 * group, 2)], y_recv.at[offset - 1, group])
        if (offset, group % 2) in ((3, 0), (1, 1)):
            step = 1 if offset == 3 else 3
            places = pl.ds(2 * group, 2)
            remote(
                got_y.at[offset - 1, places, pl.ds(0, HALF)], got_y.at[1, places, pl.ds(0, HALF)],
                relay_send.at[group], y_recv.at[1, group], at((y + step) % NY, z, core),
            ).start()
            left_with(got_y.at[0, pl.ds(0, 2), pl.ds(0, HALF)], relay_send.at[group])
        for place in (2 * group, 2 * group + 1):
            to_x(got_y.at[offset - 1, place, pl.ds(0, HALF)], offset, place)

    bins = lax.broadcasted_iota(jnp.int32, (BINS, 1), 0).astype(F32)

    def add_rows(offset, first=False, after=None):
        arrived(got_x.at[offset], x_recv.at[offset])
        if offset == 0:
            pieces = [piece(i) for i in range(NZ)]
            start = pl.multiple_of(HALF + 16 * block, 16)
            kept = [ref[0:HALF, :] for ref in pieces]
            codes = [ref[pl.ds(start, 16), :] for ref in pieces]
            weights = [got_h[i] for i in range(NZ)]
        else:
            arrived(got_yh.at[offset - 1], yh_recv.at[offset - 1])
            kept = [got_y[offset - 1, i, 0:HALF, :] for i in range(NZ)]
            codes = [got_y[offset - 1, i, HALF:GOES_Y, :] for i in range(NZ)]
            weights = [got_yh[offset - 1, i] for i in range(NZ)]
        tile = jnp.concatenate(
            [jnp.concatenate(weights, 1), jnp.zeros((15, NZ * SLOTS), F32)], 0
        ).astype(BF16)
        values = jnp.concatenate([
            jnp.concatenate(kept, 1),
            jnp.concatenate([got_x[offset, i] for i in range(NZ)], 1),
            tile,
        ], 0)
        codes_here[...] = jnp.concatenate(codes, 1).astype(F32)
        for turn, (core_to, base) in enumerate(
            ((1 - core, other), (1 - core, own), (core, other), (core, own))
        ):
            masks = []
            for i in range(2):
                high = (2 * (base + i) + 7 * core_to) % 8
                for line in (high, 8 + high):
                    masks.append(ones_where(codes_here[pl.ds(line, 1), :] <= bins))
            found = nt_dot(values, jnp.concatenate(masks, 0))
            for i in range(2):
                new = found[:KEEP, 128 * i:128 * i + 128]
                if first:
                    acc[4 * core_to + base + i] = new
                else:
                    acc[4 * core_to + base + i] += new
            if after is not None:
                after(turn)

    buddy = at(y, z, 1 - core)

    def to_buddy(turn):
        if turn < 2:
            base = (other, own)[turn]
            for i in range(2):
                remote(
                    acc.at[4 * (1 - core) + base + i], half.at[base + i],
                    core_send.at[2 * turn + i], core_recv.at[2 * turn + i], buddy,
                ).start()
                left_with(half.at[0], core_send.at[2 * turn + i])

    from_z(0)
    from_z(1)
    from_y(1, 0)
    from_y(3, 0)
    from_z(2)
    from_y(1, 1)
    from_y(3, 1)
    from_z(3)
    arrived(got_h.at[pl.ds(1, NZ - 1)], zh_recv)
    for step in range(1, NY):
        remote(
            got_h, got_yh.at[NY - step - 1], yh_send.at[step], yh_recv.at[NY - step - 1],
            at((y + step) % NY, z, core),
        ).start()
        left_with(got_h, yh_send.at[step])
    from_y(2, 0)
    from_y(1, 2)
    from_y(3, 2)
    from_y(2, 1)
    from_y(1, 3)
    from_y(3, 3)
    for step in (1, 3):
        left_with(got_y.at[0], y_send.at[step])
    left_with(got_y.at[0, pl.ds(0, NZ), pl.ds(0, 16)], y_send.at[2])
    for y_from in range(NY):
        arrived(part_y.at[y_from], py_recv.at[y_from])
    mine_z[...] = (part_y[0] + part_y[1]) + (part_y[2] + part_y[3])
    for step in range(1, NZ):
        remote(
            mine_z, part_z.at[z], pz_send.at[step], pz_recv.at[z], at(y, (z + step) % NZ, core)
        ).start()
        left_with(mine_z, pz_send.at[step])
    pltpu.make_async_copy(mine_z, part_z.at[z], pz_recv.at[z]).start()
    add_rows(0, first=True)
    from_y(2, 2)
    add_rows(1)
    from_y(2, 3)
    for side in range(2):
        left_with(got_x.at[pl.ds(0, 2)], x_send.at[side])
    add_rows(3)
    add_rows(2, after=to_buddy)

    sibling = at(y, z + 1 - 2 * (z % 2), core)
    for i in range(2):
        arrived(half.at[other + i], core_recv.at[i])
        deep[other + i] = acc[4 * core + other + i] + half[other + i]
        remote(deep.at[other + i], sib.at[i], sib_send.at[i], sib_recv.at[i], sibling).start()
        left_with(sib.at[i], sib_send.at[i])
    for i in range(2):
        arrived(half.at[own + i], core_recv.at[2 + i])
        deep[own + i] = acc[4 * core + own + i] + half[own + i]

    def hand_over(src, dst, send, recv, row_to):
        @pl.when(row_to != row)
        def _():
            remote(src, dst, send, recv, row_to).start()

        @pl.when(row_to == row)
        def _():
            pltpu.make_async_copy(src, dst, recv).start()

        def leave():
            @pl.when(row_to != row)
            def _():
                arrived(src, send)

        leaving.append(leave)

    spot3 = 2 * core + block % 2
    for i in range(4):
        gain3[i] = gains_of(deep[i])
    for i in range(4):
        row_to = 8 * z + 4 * (block // 2) + (i + 3 * core) % 4
        hand_over(gain3.at[i], home3.at[spot3], g3_send.at[i], g3_recv.at[spot3], row_to)

    for z_from in range(NZ):
        arrived(part_z.at[z_from], pz_recv.at[z_from])
    total_z = part_z[0]
    for z_from in range(1, NZ):
        total_z = total_z + part_z[z_from]
    mine_x[...] = total_z
    here = 2 * x + core
    for step in range(1, 2 * NX):
        remote(
            mine_x, part_x.at[here], px_send.at[step], px_recv.at[here],
            at(y, z, (core + step) % 2), (x + step // 2) % NX,
        ).start()
        left_with(mine_x, px_send.at[step])
    pltpu.make_async_copy(mine_x, part_x.at[here], px_recv.at[here]).start()

    high_bits = [(2 * (own + i) + 7 * core) % 8 for i in range(2)]
    which1 = (z // 2) % 2
    for i in range(2):
        arrived(sib.at[i], sib_recv.at[i])
        mid[i] = deep[own + i] + sib[i]
        hand_over(
            mid.at[i], low.at[which1], low_send.at[i], low_recv.at[which1],
            at(2 * upper + block // 2, high_bits[i], block % 2),
        )
    spot2 = block % 2
    for i in range(2):
        gain2[i] = gains_of(mid[i])
        hand_over(
            gain2.at[i], home2.at[spot2], g2_send.at[i], g2_recv.at[spot2],
            16 * (z // 2) + 8 * (block // 2) + high_bits[i],
        )

    for i in range(4):
        arrived(home3.at[i], g3_recv.at[i])
        three_ref[2 * i:2 * i + 1, :] = home3[i, :, 0:64]
        three_ref[2 * i + 1:2 * i + 2, :] = home3[i, :, 64:128]

    for i in range(2 * NX):
        arrived(part_x.at[i], px_recv.at[i])
    total_x = part_x[0]
    for i in range(1, 2 * NX):
        total_x = total_x + part_x[i]
    scores = -total_x[0:8] / jnp.sqrt(total_x[8:16] + penalty)
    child_out[0, 0] = scores[0:2]
    child_out[1, 0] = scores[2:4]
    child_out[2, 0] = jnp.where(z < NZ // 2, scores[4:6], scores[6:8])

    for i in range(2):
        arrived(low.at[i], low_recv.at[i])
    last = gains_of(low[0] + low[1])
    one_ref[0:1, :] = last[:, 0:64]
    one_ref[1:2, :] = last[:, 64:128]
    for i in range(2):
        arrived(home2.at[i], g2_recv.at[i])
        two_ref[2 * i:2 * i + 1, :] = home2[i, :, 0:64]
        two_ref[2 * i + 1:2 * i + 2, :] = home2[i, :, 64:128]

    for leave in leaving:
        leave()


def on_device(gradients, hessians, bin_words, children, split_feature, split_bin):
    dma = pltpu.SemaphoreType.DMA
    vmem = pl.BlockSpec(memory_space=pltpu.VMEM)
    return pl.pallas_call(
        kernel,
        out_shape=(
            jax.ShapeDtypeStruct((2, BINS), F32),
            jax.ShapeDtypeStruct((4, BINS), F32),
            jax.ShapeDtypeStruct((8, BINS), F32),
            jax.ShapeDtypeStruct((LEVELS, 1, 2, OUT), F32),
        ),
        in_specs=[pl.BlockSpec(memory_space=pl.ANY)] * 6,
        out_specs=(vmem,) * 4,
        scratch_shapes=[
            pltpu.SMEM((SPLITS,), jnp.int32),
            pltpu.SMEM((SPLITS,), jnp.int32),
            pltpu.VMEM((ROW_DEV, OUT), BF16),
            pltpu.VMEM((ROW_DEV,), BF16),
            pltpu.VMEM((32, ROW_DEV), jnp.int32),
            pltpu.VMEM((LEVELS, ROW_DEV), jnp.int32),
            pltpu.VMEM((NZ, PIECE, SLOTS), BF16),
            pltpu.VMEM((NZ, 1, SLOTS), F32),
            pltpu.VMEM((NZ - 1, PIECE, SLOTS), BF16),
            pltpu.VMEM((NZ, 1, SLOTS), F32),
            pltpu.VMEM((NY - 1, NZ, GOES_Y, SLOTS), BF16),
            pltpu.VMEM((NY - 1, NZ, 1, SLOTS), F32),
            pltpu.VMEM((NY, NZ, HALF, SLOTS), BF16),
            pltpu.VMEM((16, NZ * SLOTS), F32),
            pltpu.VMEM((8, KEEP, 128), F32),
            pltpu.VMEM((4, KEEP, 128), F32),
            pltpu.VMEM((4, KEEP, 128), F32),
            pltpu.VMEM((2, KEEP, 128), F32),
            pltpu.VMEM((2, KEEP, 128), F32),
            pltpu.VMEM((2, KEEP, 128), F32),
            pltpu.VMEM((4, 1, 128), F32),
            pltpu.VMEM((4, 1, 128), F32),
            pltpu.VMEM((2, 1, 128), F32),
            pltpu.VMEM((2, 1, 128), F32),
            pltpu.VMEM((NY, 16, 128), F32),
            pltpu.VMEM((NY, 16, 128), F32),
            pltpu.VMEM((16, 128), F32),
            pltpu.VMEM((NZ, 16, 128), F32),
            pltpu.VMEM((16, 128), F32),
            pltpu.VMEM((2 * NX, 16, 128), F32),
            dma((6,)), dma((NZ,)), dma((NZ,)), dma, dma, dma((NY,)), dma((NY - 1, 4)),
            dma((NY,)), dma((NY - 1,)), dma((4,)), dma((2,)), dma((NY,)),
            dma((4,)), dma((4,)), dma((2,)), dma((2,)),
            dma((2,)), dma((2,)), dma((4,)), dma((4,)), dma((2,)), dma((2,)),
            dma((NY,)), dma((NY,)), dma((NZ,)), dma((NZ,)), dma((2 * NX,)), dma((2 * NX,)),
        ],
        compiler_params=pltpu.CompilerParams(collective_id=0, has_side_effects=True),
    )(split_feature, split_bin, gradients, hessians, bin_words, children)


def solution(mesh):
    placed = (P("rows", None), P("rows"), P("feat", "rows"), P(None, "rows"), P(), P())
    return jax.shard_map(
        on_device,
        mesh=mesh,
        in_specs=placed,
        out_specs=(
            P("rows", "feat"),
            P("rows", "feat"),
            P("rows", "feat"),
            P(None, "rows", None, None),
        ),
        check_vma=False,
    )
```

time: 57.4 us -> 48.2 us (0.84)
  Pallas kernels: 50.8 us -> 44.3 us
  local copies, waits for them, and re-layouts: 5.45 us -> 3.04 us
    pallas_call x1, Pallas kernels: 50.8 us -> 44.3 us  [on_device(): pl.pallas_call(kernel, out_shape=(jax.ShapeDtypeStruct((2, BINS), F32), j...]
    unnamed x14 -> x12, local copies, waits for them, and re-layouts: 4.75 us -> 3.04 us
    reshape x1 -> x0, local copies, waits for them, and re-layouts: 0.69 us -> none  [on_device(): hessians.reshape(1, -1)]
where the time goes in v2:
time: 48.2 us; the launch traced here: 48 us
  Pallas kernels  44.3 us (92%)
  local copies, waits for them, and re-layouts  3.04 us (6%)
  between operations  0.67 us (1%)
    pallas_call x1, Pallas kernels, on_device(): pl.pallas_call(kernel, out_shape=(jax.ShapeDtypeStruct((2, BINS), F32), j...  44.3 us
    unnamed x12, local copies, waits for them, and re-layouts  3.04 us

profile of v2, /device:TPU:1, one launch (start us, length us, event | category | flops | bytes accessed | tf_op | source)
XLA Modules:
  0.0 48.0 jit_solution(15096903488722449317)
XLA Ops:
  0.6 44.3 %shard_map.93 = (f32[2,64]{1,0:T(2,128)}, f32[4,64]{1,0:T(4,128)}, f32[8,64]{1,0:T(8,128)}, f32[3,1,2,128]{3,2,1,0:T(2,128)}) custom-call(s32[14]{0:T(128)} %split_feature_any.1, s32[14]{0:T(128)} %split_bin_any.1, bf16[512,128]{1,0:T(8,128)(2,1)} %grad_any.1, bf16[512]{0:T(512)(128)(2,1)} %hess_any.1, s32[32,512]{1,0:T(8,128)} %word_any.1, s32[3,512]{1,0:T(4,128)} %child_any.1), custom_call_target="tpu_custom_call" | custom-call | tf_op jit(solution)/shard_map/pallas_call | solution.py:446
  45.0 0.0 copy-start.3
  45.0 0.0 copy-start.2
  45.0 0.0 copy-start
  45.0 0.6 %copy-done.3 = f32[2,64]{1,0:T(2,128)S(1)} copy-done((f32[2,64]{1,0:T(2,128)S(1)}, f32[2,64]{1,0:T(2,128)}, u32[]{:S(2)}) %copy-start.3) | copy-done | bytes 536
  45.6 0.6 %copy.14 = f32[2,64]{1,0:T(2,128)} copy(f32[2,64]{1,0:T(2,128)S(1)} %copy-done.3) | data formatting | bytes 1024
  46.2 0.0 copy-done.2
  46.2 0.6 %copy.15 = f32[4,64]{1,0:T(4,128)} copy(f32[4,64]{1,0:T(4,128)S(1)} %copy-done.2) | data formatting | bytes 2048
  46.8 0.0 copy-done
  46.8 0.0 copy-start.1
  46.8 0.6 %copy.16 = f32[8,64]{1,0:T(8,128)} copy(f32[8,64]{1,0:T(8,128)S(1)} %copy-done) | data formatting | bytes 4096
  47.4 0.1 copy-done.1
  47.5 0.6 %copy.17 = f32[3,1,2,128]{3,2,1,0:T(2,128)} copy(f32[3,1,2,128]{3,2,1,0:T(2,128)S(1)} %copy-done.1) | data formatting | bytes 6144
Async XLA Ops:
  45.0 0.7 %copy-start.3 = (f32[2,64]{1,0:T(2,128)S(1)}, f32[2,64]{1,0:T(2,128)}, u32[]{:S(2)}) copy-start(f32[2,64]{1,0:T(2,128)} %get-tuple-element.8) | copy-start | bytes 1540
  45.0 1.2 %copy-start.2 = (f32[4,64]{1,0:T(4,128)S(1)}, f32[4,64]{1,0:T(4,128)}, u32[]{:S(2)}) copy-start(f32[4,64]{1,0:T(4,128)} %get-tuple-element.9) | copy-start | bytes 3076
  45.0 1.8 %copy-start = (f32[8,64]{1,0:T(8,128)S(1)}, f32[8,64]{1,0:T(8,128)}, u32[]{:S(2)}) copy-start(f32[8,64]{1,0:T(8,128)} %get-tuple-element.10) | copy-start | bytes 6148
  46.8 0.7 %copy-start.1 = (f32[3,1,2,128]{3,2,1,0:T(2,128)S(1)}, f32[3,1,2,128]{3,2,1,0:T(2,128)}, u32[]{:S(2)}) copy-start(f32[3,1,2,128]{3,2,1,0:T(2,128)} %get-tuple-element.11) | copy-start | bytes 9220

commit v3 on v2

--- a/solution.py
+++ b/solution.py
@@ -21,6 +21,7 @@
 BF16 = jnp.bfloat16
 
 penalty = 1.0
+DIRECT = (3,)
 NEAR = (0, 1, 7, 2, 6, 3, 5, 4)
 
 
@@ -50,7 +51,7 @@
 
 def kernel(
     split_feature_any, split_bin_any, grad_any, hess_any, word_any, child_any,
-    one_ref, two_ref, three_ref, child_out,
+    out_ref,
     split_feature, split_bin, grad_ref, hess_ref, word_ref, child_ref,
     sent, sent_h, got_z, got_h, got_y, got_yh, got_x, codes_here,
     acc, half, deep, sib, mid, low,
@@ -214,7 +215,8 @@
     def to_x(src, offset, place):
         step = 1 - 2 * (place % 2)
         remote(
-            src, got_x.at[offset, place], x_send.at[place % 2], x_recv.at[offset],
+            src, got_x.at[offset, place], x_send.at[place % 2],
+            x_recv.at[offset + 2 * int(offset == 2 and place >= NZ // 2)],
             row, (x + step) % NX,
         ).start()
 
@@ -223,10 +225,11 @@
             if place:
                 arrived(got_z.at[place - 1], z_recv.at[place])
             here = piece(place)
-            for step in (1, 3):
+            for step in (1, 3, 2) if group in DIRECT else (1, 3):
                 remote(
                     here.at[pl.ds(0, HALF)], got_y.at[NY - step - 1, place, pl.ds(0, HALF)],
-                    y_send.at[step], y_recv.at[NY - step - 1, group], at((y + step) % NY, z, core),
+                    y_send.at[step % 2 * step], y_recv.at[NY - step - 1, group],
+                    at((y + step) % NY, z, core),
                 ).start()
             for step in (1, 3, 2):
                 y_to = (y + step) % NY
@@ -239,7 +242,7 @@
 
     def from_y(offset, group):
         arrived(got_y.at[offset - 1, pl.ds(2 * group, 2)], y_recv.at[offset - 1, group])
-        if (offset, group % 2) in ((3, 0), (1, 1)):
+        if group not in DIRECT and (offset, group % 2) in ((3, 0), (1, 1)):
             step = 1 if offset == 3 else 3
             places = pl.ds(2 * group, 2)
             remote(
@@ -252,36 +255,39 @@
 
     bins = lax.broadcasted_iota(jnp.int32, (BINS, 1), 0).astype(F32)
 
-    def add_rows(offset, first=False, after=None):
-        arrived(got_x.at[offset], x_recv.at[offset])
+    def add_rows(offset, first=False, after=None, places=range(NZ)):
+        here_x = pl.ds(places[0], len(places))
+        late = int(offset == 2 and places[0] > 0)
+        arrived(got_x.at[offset, here_x], x_recv.at[offset + 2 * late])
         if offset == 0:
-            pieces = [piece(i) for i in range(NZ)]
+            pieces = [piece(i) for i in places]
             start = pl.multiple_of(HALF + 16 * block, 16)
             kept = [ref[0:HALF, :] for ref in pieces]
             codes = [ref[pl.ds(start, 16), :] for ref in pieces]
-            weights = [got_h[i] for i in range(NZ)]
+            weights = [got_h[i] for i in places]
         else:
-            arrived(got_yh.at[offset - 1], yh_recv.at[offset - 1])
-            kept = [got_y[offset - 1, i, 0:HALF, :] for i in range(NZ)]
-            codes = [got_y[offset - 1, i, HALF:GOES_Y, :] for i in range(NZ)]
-            weights = [got_yh[offset - 1, i] for i in range(NZ)]
+            if not late:
+                arrived(got_yh.at[offset - 1], yh_recv.at[offset - 1])
+            kept = [got_y[offset - 1, i, 0:HALF, :] for i in places]
+            codes = [got_y[offset - 1, i, HALF:GOES_Y, :] for i in places]
+            weights = [got_yh[offset - 1, i] for i in places]
         tile = jnp.concatenate(
-            [jnp.concatenate(weights, 1), jnp.zeros((15, NZ * SLOTS), F32)], 0
+            [jnp.concatenate(weights, 1), jnp.zeros((15, len(places) * SLOTS), F32)], 0
         ).astype(BF16)
         values = jnp.concatenate([
             jnp.concatenate(kept, 1),
-            jnp.concatenate([got_x[offset, i] for i in range(NZ)], 1),
+            jnp.concatenate([got_x[offset, i] for i in places], 1),
             tile,
         ], 0)
-        codes_here[...] = jnp.concatenate(codes, 1).astype(F32)
+        codes_here[:, 0:len(places) * SLOTS] = jnp.concatenate(codes, 1).astype(F32)
         for turn, (core_to, base) in enumerate(
             ((1 - core, other), (1 - core, own), (core, other), (core, own))
         ):
             masks = []
             for i in range(2):
-                high = (2 * (base + i) + 7 * core_to) % 8
+                high = (2 * (base + i) + 5 * core_to) % 8
                 for line in (high, 8 + high):
-                    masks.append(ones_where(codes_here[pl.ds(line, 1), :] <= bins))
+                    masks.append(ones_where(codes_here[pl.ds(line, 1), 0:len(places) * SLOTS] <= bins))
             found = nt_dot(values, jnp.concatenate(masks, 0))
             for i in range(2):
                 new = found[:KEEP, 128 * i:128 * i + 128]
@@ -306,28 +312,27 @@
 
     from_z(0)
     from_z(1)
+    from_z(2)
     from_y(1, 0)
     from_y(3, 0)
-    from_z(2)
     from_y(1, 1)
     from_y(3, 1)
     from_z(3)
-    arrived(got_h.at[pl.ds(1, NZ - 1)], zh_recv)
-    for step in range(1, NY):
-        remote(
-            got_h, got_yh.at[NY - step - 1], yh_send.at[step], yh_recv.at[NY - step - 1],
-            at((y + step) % NY, z, core),
-        ).start()
-        left_with(got_h, yh_send.at[step])
     from_y(2, 0)
     from_y(1, 2)
     from_y(3, 2)
     from_y(2, 1)
     from_y(1, 3)
     from_y(3, 3)
-    for step in (1, 3):
-        left_with(got_y.at[0], y_send.at[step])
-    left_with(got_y.at[0, pl.ds(0, NZ), pl.ds(0, 16)], y_send.at[2])
+    arrived(got_h.at[pl.ds(1, NZ - 1)], zh_recv)
+    for step in range(1, NY):
+        remote(
+            got_h, got_yh.at[NY - step - 1], yh_send.at[step], yh_recv.at[NY - step - 1],
+            at((y + step) % NY, z, core),
+        ).start()
+        left_with(got_h, yh_send.at[step])
+    from_y(2, 2)
+    from_y(2, 3)
     for y_from in range(NY):
         arrived(part_y.at[y_from], py_recv.at[y_from])
     mine_z[...] = (part_y[0] + part_y[1]) + (part_y[2] + part_y[3])
@@ -337,14 +342,17 @@
         ).start()
         left_with(mine_z, pz_send.at[step])
     pltpu.make_async_copy(mine_z, part_z.at[z], pz_recv.at[z]).start()
+    for step in (1, 3):
+        left_with(got_y.at[0], y_send.at[step])
+    left_with(got_y.at[0, pl.ds(0, NZ), pl.ds(0, 16)], y_send.at[2])
+    left_with(got_y.at[0, pl.ds(0, 2 * len(DIRECT)), pl.ds(0, HALF)], y_send.at[0])
     add_rows(0, first=True)
-    from_y(2, 2)
     add_rows(1)
-    from_y(2, 3)
     for side in range(2):
         left_with(got_x.at[pl.ds(0, 2)], x_send.at[side])
     add_rows(3)
-    add_rows(2, after=to_buddy)
+    add_rows(2, places=range(NZ // 2))
+    add_rows(2, after=to_buddy, places=range(NZ // 2, NZ))
 
     sibling = at(y, z + 1 - 2 * (z % 2), core)
     for i in range(2):
@@ -376,7 +384,7 @@
     for i in range(4):
         gain3[i] = gains_of(deep[i])
     for i in range(4):
-        row_to = 8 * z + 4 * (block // 2) + (i + 3 * core) % 4
+        row_to = 8 * z + 4 * (block // 2) + (i + 2 * core) % 4
         hand_over(gain3.at[i], home3.at[spot3], g3_send.at[i], g3_recv.at[spot3], row_to)
 
     for z_from in range(NZ):
@@ -394,7 +402,7 @@
         left_with(mine_x, px_send.at[step])
     pltpu.make_async_copy(mine_x, part_x.at[here], px_recv.at[here]).start()
 
-    high_bits = [(2 * (own + i) + 7 * core) % 8 for i in range(2)]
+    high_bits = [(2 * (own + i) + 5 * core) % 8 for i in range(2)]
     which1 = (z // 2) % 2
     for i in range(2):
         arrived(sib.at[i], sib_recv.at[i])
@@ -413,8 +421,7 @@
 
     for i in range(4):
         arrived(home3.at[i], g3_recv.at[i])
-        three_ref[2 * i:2 * i + 1, :] = home3[i, :, 0:64]
-        three_ref[2 * i + 1:2 * i + 2, :] = home3[i, :, 64:128]
+        out_ref[i:i + 1, :] = home3[i]
 
     for i in range(2 * NX):
         arrived(part_x.at[i], px_recv.at[i])
@@ -422,37 +429,38 @@
     for i in range(1, 2 * NX):
         total_x = total_x + part_x[i]
     scores = -total_x[0:8] / jnp.sqrt(total_x[8:16] + penalty)
-    child_out[0, 0] = scores[0:2]
-    child_out[1, 0] = scores[2:4]
-    child_out[2, 0] = jnp.where(z < NZ // 2, scores[4:6], scores[6:8])
+    out_ref[8:12, :] = scores[0:4]
+    out_ref[12:14, :] = jnp.where(z < NZ // 2, scores[4:6], scores[6:8])
 
     for i in range(2):
         arrived(low.at[i], low_recv.at[i])
     last = gains_of(low[0] + low[1])
-    one_ref[0:1, :] = last[:, 0:64]
-    one_ref[1:2, :] = last[:, 64:128]
+    out_ref[6:7, :] = last
     for i in range(2):
         arrived(home2.at[i], g2_recv.at[i])
-        two_ref[2 * i:2 * i + 1, :] = home2[i, :, 0:64]
-        two_ref[2 * i + 1:2 * i + 2, :] = home2[i, :, 64:128]
+        out_ref[4 + i:5 + i, :] = home2[i]
 
     for leave in leaving:
         leave()
+
+
+def spread(all_ref, one_ref, two_ref, three_ref, child_out):
+    for first, ref in ((0, three_ref), (4, two_ref), (6, one_ref)):
+        for i in range(ref.shape[0] // 2):
+            ref[2 * i:2 * i + 1, :] = all_ref[first + i:first + i + 1, 0:BINS]
+            ref[2 * i + 1:2 * i + 2, :] = all_ref[first + i:first + i + 1, BINS:2 * BINS]
+    for level in range(LEVELS):
+        child_out[level, 0] = all_ref[8 + 2 * level:10 + 2 * level, :]
 
 
 def on_device(gradients, hessians, bin_words, children, split_feature, split_bin):
     dma = pltpu.SemaphoreType.DMA
     vmem = pl.BlockSpec(memory_space=pltpu.VMEM)
-    return pl.pallas_call(
+    together = pl.pallas_call(
         kernel,
-        out_shape=(
-            jax.ShapeDtypeStruct((2, BINS), F32),
-            jax.ShapeDtypeStruct((4, BINS), F32),
-            jax.ShapeDtypeStruct((8, BINS), F32),
-            jax.ShapeDtypeStruct((LEVELS, 1, 2, OUT), F32),
-        ),
+        out_shape=jax.ShapeDtypeStruct((16, 128), F32),
         in_specs=[pl.BlockSpec(memory_space=pl.ANY)] * 6,
-        out_specs=(vmem,) * 4,
+        out_specs=vmem,
         scratch_shapes=[
             pltpu.SMEM((SPLITS,), jnp.int32),
             pltpu.SMEM((SPLITS,), jnp.int32),
@@ -485,13 +493,24 @@
             pltpu.VMEM((16, 128), F32),
             pltpu.VMEM((2 * NX, 16, 128), F32),
             dma((6,)), dma((NZ,)), dma((NZ,)), dma, dma, dma((NY,)), dma((NY - 1, 4)),
-            dma((NY,)), dma((NY - 1,)), dma((4,)), dma((2,)), dma((NY,)),
+            dma((NY,)), dma((NY - 1,)), dma((4,)), dma((2,)), dma((NY + 1,)),
             dma((4,)), dma((4,)), dma((2,)), dma((2,)),
             dma((2,)), dma((2,)), dma((4,)), dma((4,)), dma((2,)), dma((2,)),
             dma((NY,)), dma((NY,)), dma((NZ,)), dma((NZ,)), dma((2 * NX,)), dma((2 * NX,)),
         ],
         compiler_params=pltpu.CompilerParams(collective_id=0, has_side_effects=True),
     )(split_feature, split_bin, gradients, hessians, bin_words, children)
+    return pl.pallas_call(
+        spread,
+        out_shape=(
+            jax.ShapeDtypeStruct((2, BINS), F32),
+            jax.ShapeDtypeStruct((4, BINS), F32),
+            jax.ShapeDtypeStruct((8, BINS), F32),
+            jax.ShapeDtypeStruct((LEVELS, 1, 2, OUT), F32),
+        ),
+        in_specs=[vmem],
+        out_specs=(vmem,) * 4,
+    )(together)
 
 
 def solution(mesh):

time: 48.2 us -> 44.9 us (0.932)
  local copies, waits for them, and re-layouts: 3.04 us -> 0 us
    unnamed x12 -> x0, local copies, waits for them, and re-layouts: 3.04 us -> none
    pallas_call x1 -> x2, Pallas kernels: 44.3 us -> 44 us  [the longest x1 42.6 us: on_device(): pl.pallas_call(kernel, out_shape=jax.ShapeDtypeStruct((16, 128), F32), in...]
where the time goes in v3:
time: 44.9 us; the launch traced here: 44.6 us
  Pallas kernels  44 us (98%)
  between operations  0.64 us (1%)
    pallas_call x1, Pallas kernels, on_device(): pl.pallas_call(kernel, out_shape=jax.ShapeDtypeStruct((16, 128), F32), in...  42.6 us
    pallas_call x1, Pallas kernels, on_device(): pl.pallas_call(spread, out_shape=(jax.ShapeDtypeStruct((2, BINS), F32), j...  1.37 us

profile of v3, /device:TPU:1, one launch (start us, length us, event | category | flops | bytes accessed | tf_op | source)
XLA Modules:
  0.0 44.6 jit_solution(1056674011239693579)
XLA Ops:
  0.6 42.6 %shard_map.93.all_ref = f32[16,128]{1,0:T(8,128)} custom-call(s32[14]{0:T(128)} %split_feature_any.1, s32[14]{0:T(128)} %split_bin_any.1, bf16[512,128]{1,0:T(8,128)(2,1)} %grad_any.1, bf16[512]{0:T(512)(128)(2,1)} %hess_any.1, s32[32,512]{1,0:T(8,128)} %word_any.1, s32[3,512]{1,0:T(4,128)} %child_any.1), custom_call_target="tpu_custom_call" | custom-call | tf_op jit(solution)/shard_map/pallas_call | solution.py:459
  43.3 1.4 %shard_map.94 = (f32[2,64]{1,0:T(2,128)}, f32[4,64]{1,0:T(4,128)}, f32[8,64]{1,0:T(8,128)}, f32[3,1,2,128]{3,2,1,0:T(2,128)}) custom-call(f32[16,128]{1,0:T(8,128)} %shard_map.93.all_ref), custom_call_target="tpu_custom_call" | custom-call | tf_op jit(solution)/shard_map/pallas_call | solution.py:503

commit v4 on v3

--- a/solution.py
+++ b/solution.py
@@ -21,8 +21,8 @@
 BF16 = jnp.bfloat16
 
 penalty = 1.0
-DIRECT = (3,)
-NEAR = (0, 1, 7, 2, 6, 3, 5, 4)
+DIRECT = (0, 1, 2, 3)
+NEAR = (0, 1, 7, 2, 6, 4, 3, 5)
 
 
 def block_of(y, upper):
@@ -57,7 +57,7 @@
     acc, half, deep, sib, mid, low,
     gain3, home3, gain2, home2, part, part_y, mine_z, part_z, mine_x, part_x,
     in_sem, z_send, z_recv, zh_send, zh_recv, y_send, y_recv, yh_send, yh_recv,
-    relay_send, x_send, x_recv, core_send, core_recv, sib_send, sib_recv,
+    x_send, x_recv, core_send, core_recv, sib_send, sib_recv,
     low_send, low_recv, g3_send, g3_recv, g2_send, g2_recv,
     py_send, py_recv, pz_send, pz_recv, px_send, px_recv,
 ):
@@ -107,6 +107,9 @@
         greet(at(y, (z + step) % NZ, core), x)
     for step in (2, 1, 3):
         greet(at((y + step) % NY, z, core), x)
+    for step in (2, 1, 3):
+        for side in (1, NX - 1):
+            greet(at((y + step) % NY, z, core), (x + side) % NX)
     for step in range(1, 2 * NX):
         greet(at(y, z, (core + step) % 2), (x + step // 2) % NX)
     for copy in inputs:
@@ -152,15 +155,15 @@
             sent_h[2 * pair + side] = chosen[PIECE:PIECE + 1, lanes]
     got_h[0] = sent_h[z]
 
-    pl.semaphore_wait(barrier, (NZ - 1) + (NY - 1) + (2 * NX - 1))
-    for step in (1, 7, 2, 6, 3, 5, 4):
+    pl.semaphore_wait(barrier, (NZ - 1) + 3 * (NY - 1) + (2 * NX - 1))
+    for step in (1, 7, 4, 2, 6, 3, 5):
         z_to = (z + step) % NZ
         place = NEAR.index((NZ - step) % NZ)
         remote(
             sent.at[z_to], got_z.at[place - 1], z_send.at[step], z_recv.at[place], at(y, z_to, core)
         ).start()
         left_with(sent.at[step], z_send.at[step])
-    for step in (1, 7, 2, 6, 3, 5, 4):
+    for step in (1, 7, 4, 2, 6, 3, 5):
         z_to = (z + step) % NZ
         place = NEAR.index((NZ - step) % NZ)
         remote(
@@ -212,12 +215,12 @@
     def piece(place):
         return sent.at[z] if place == 0 else got_z.at[place - 1]
 
-    def to_x(src, offset, place):
+    def to_x(src, offset, place, y_step=0):
         step = 1 - 2 * (place % 2)
-        remote(
-            src, got_x.at[offset, place], x_send.at[place % 2],
-            x_recv.at[offset + 2 * int(offset == 2 and place >= NZ // 2)],
-            row, (x + step) % NX,
+        late = int(place >= NZ // 2)
+        remote(
+            src, got_x.at[offset, place], x_send.at[place % 2], x_recv.at[offset, late],
+            at((y + y_step) % NY, z, core), (x + step) % NX,
         ).start()
 
     def from_z(group):
@@ -225,10 +228,10 @@
             if place:
                 arrived(got_z.at[place - 1], z_recv.at[place])
             here = piece(place)
-            for step in (1, 3, 2) if group in DIRECT else (1, 3):
+            for step in (1, 3, 2):
                 remote(
                     here.at[pl.ds(0, HALF)], got_y.at[NY - step - 1, place, pl.ds(0, HALF)],
-                    y_send.at[step % 2 * step], y_recv.at[NY - step - 1, group],
+                    y_send.at[step], y_recv.at[NY - step - 1, group],
                     at((y + step) % NY, z, core),
                 ).start()
             for step in (1, 3, 2):
@@ -238,27 +241,20 @@
                     here.at[pl.ds(start, 16)], got_y.at[NY - step - 1, place, pl.ds(HALF, 16)],
                     y_send.at[step], y_recv.at[NY - step - 1, group], at(y_to, z, core),
                 ).start()
-            to_x(here.at[pl.ds(0, HALF)], 0, place)
+            for step in (0, 1, 3, 2) if group in DIRECT else (0,):
+                to_x(here.at[pl.ds(0, HALF)], (NY - step) % NY, place, step)
 
     def from_y(offset, group):
         arrived(got_y.at[offset - 1, pl.ds(2 * group, 2)], y_recv.at[offset - 1, group])
-        if group not in DIRECT and (offset, group % 2) in ((3, 0), (1, 1)):
-            step = 1 if offset == 3 else 3
-            places = pl.ds(2 * group, 2)
-            remote(
-                got_y.at[offset - 1, places, pl.ds(0, HALF)], got_y.at[1, places, pl.ds(0, HALF)],
-                relay_send.at[group], y_recv.at[1, group], at((y + step) % NY, z, core),
-            ).start()
-            left_with(got_y.at[0, pl.ds(0, 2), pl.ds(0, HALF)], relay_send.at[group])
-        for place in (2 * group, 2 * group + 1):
+        for place in (2 * group, 2 * group + 1) if group not in DIRECT else ():
             to_x(got_y.at[offset - 1, place, pl.ds(0, HALF)], offset, place)
 
     bins = lax.broadcasted_iota(jnp.int32, (BINS, 1), 0).astype(F32)
 
     def add_rows(offset, first=False, after=None, places=range(NZ)):
         here_x = pl.ds(places[0], len(places))
-        late = int(offset == 2 and places[0] > 0)
-        arrived(got_x.at[offset, here_x], x_recv.at[offset + 2 * late])
+        late = int(places[0] > 0)
+        arrived(got_x.at[offset, here_x], x_recv.at[offset, late])
         if offset == 0:
             pieces = [piece(i) for i in places]
             start = pl.multiple_of(HALF + 16 * block, 16)
@@ -313,17 +309,7 @@
     from_z(0)
     from_z(1)
     from_z(2)
-    from_y(1, 0)
-    from_y(3, 0)
-    from_y(1, 1)
-    from_y(3, 1)
     from_z(3)
-    from_y(2, 0)
-    from_y(1, 2)
-    from_y(3, 2)
-    from_y(2, 1)
-    from_y(1, 3)
-    from_y(3, 3)
     arrived(got_h.at[pl.ds(1, NZ - 1)], zh_recv)
     for step in range(1, NY):
         remote(
@@ -331,8 +317,6 @@
             at((y + step) % NY, z, core),
         ).start()
         left_with(got_h, yh_send.at[step])
-    from_y(2, 2)
-    from_y(2, 3)
     for y_from in range(NY):
         arrived(part_y.at[y_from], py_recv.at[y_from])
     mine_z[...] = (part_y[0] + part_y[1]) + (part_y[2] + part_y[3])
@@ -342,17 +326,30 @@
         ).start()
         left_with(mine_z, pz_send.at[step])
     pltpu.make_async_copy(mine_z, part_z.at[z], pz_recv.at[z]).start()
-    for step in (1, 3):
+    from_y(1, 0)
+    from_y(1, 1)
+    add_rows(0, first=True, places=range(NZ // 2))
+    add_rows(1, places=range(NZ // 2))
+    from_y(3, 0)
+    from_y(3, 1)
+    add_rows(3, places=range(NZ // 2))
+    from_y(2, 0)
+    from_y(2, 1)
+    add_rows(2, places=range(NZ // 2))
+    add_rows(0, places=range(NZ // 2, NZ))
+    from_y(1, 2)
+    from_y(1, 3)
+    add_rows(1, places=range(NZ // 2, NZ))
+    from_y(3, 2)
+    from_y(3, 3)
+    add_rows(3, places=range(NZ // 2, NZ))
+    from_y(2, 2)
+    from_y(2, 3)
+    add_rows(2, places=range(NZ // 2, NZ), after=to_buddy)
+    for step in range(1, NY):
         left_with(got_y.at[0], y_send.at[step])
-    left_with(got_y.at[0, pl.ds(0, NZ), pl.ds(0, 16)], y_send.at[2])
-    left_with(got_y.at[0, pl.ds(0, 2 * len(DIRECT)), pl.ds(0, HALF)], y_send.at[0])
-    add_rows(0, first=True)
-    add_rows(1)
     for side in range(2):
         left_with(got_x.at[pl.ds(0, 2)], x_send.at[side])
-    add_rows(3)
-    add_rows(2, places=range(NZ // 2))
-    add_rows(2, after=to_buddy, places=range(NZ // 2, NZ))
 
     sibling = at(y, z + 1 - 2 * (z % 2), core)
     for i in range(2):
@@ -493,7 +490,7 @@
             pltpu.VMEM((16, 128), F32),
             pltpu.VMEM((2 * NX, 16, 128), F32),
             dma((6,)), dma((NZ,)), dma((NZ,)), dma, dma, dma((NY,)), dma((NY - 1, 4)),
-            dma((NY,)), dma((NY - 1,)), dma((4,)), dma((2,)), dma((NY + 1,)),
+            dma((NY,)), dma((NY - 1,)), dma((2,)), dma((NY, 2)),
             dma((4,)), dma((4,)), dma((2,)), dma((2,)),
             dma((2,)), dma((2,)), dma((4,)), dma((4,)), dma((2,)), dma((2,)),
             dma((NY,)), dma((NY,)), dma((NZ,)), dma((NZ,)), dma((2 * NX,)), dma((2 * NX,)),

time: 44.9 us -> 44 us (0.980)
  Pallas kernels: 44 us -> 43.1 us
    pallas_call x1, Pallas kernels: 42.6 us -> 41.7 us  [on_device(): pl.pallas_call(kernel, out_shape=jax.ShapeDtypeStruct((16, 128), F32), in...]
where the time goes in v4:
time: 44 us; the launch traced here: 43.7 us
  Pallas kernels  43.1 us (98%)
  between operations  0.64 us (1%)
    pallas_call x1, Pallas kernels, on_device(): pl.pallas_call(kernel, out_shape=jax.ShapeDtypeStruct((16, 128), F32), in...  41.7 us
    pallas_call x1, Pallas kernels, on_device(): pl.pallas_call(spread, out_shape=(jax.ShapeDtypeStruct((2, BINS), F32), j...  1.37 us

profile of v4, /device:TPU:1, one launch (start us, length us, event | category | flops | bytes accessed | tf_op | source)
XLA Modules:
  0.0 43.7 jit_solution(1934897885643976591)
XLA Ops:
  0.6 41.7 %shard_map.93.all_ref = f32[16,128]{1,0:T(8,128)} custom-call(s32[14]{0:T(128)} %split_feature_any.1, s32[14]{0:T(128)} %split_bin_any.1, bf16[512,128]{1,0:T(8,128)(2,1)} %grad_any.1, bf16[512]{0:T(512)(128)(2,1)} %hess_any.1, s32[32,512]{1,0:T(8,128)} %word_any.1, s32[3,512]{1,0:T(4,128)} %child_any.1), custom_call_target="tpu_custom_call" | custom-call | tf_op jit(solution)/shard_map/pallas_call | solution.py:456
  42.4 1.4 %shard_map.94 = (f32[2,64]{1,0:T(2,128)}, f32[4,64]{1,0:T(4,128)}, f32[8,64]{1,0:T(8,128)}, f32[3,1,2,128]{3,2,1,0:T(2,128)}) custom-call(f32[16,128]{1,0:T(8,128)} %shard_map.93.all_ref), custom_call_target="tpu_custom_call" | custom-call | tf_op jit(solution)/shard_map/pallas_call | solution.py:500

commit v5 on v4

--- a/solution.py
+++ b/solution.py
@@ -455,7 +455,7 @@
     vmem = pl.BlockSpec(memory_space=pltpu.VMEM)
     together = pl.pallas_call(
         kernel,
-        out_shape=jax.ShapeDtypeStruct((16, 128), F32),
+        out_shape=pltpu.VMEM((16, 128), F32),
         in_specs=[pl.BlockSpec(memory_space=pl.ANY)] * 6,
         out_specs=vmem,
         scratch_shapes=[
@@ -497,6 +497,7 @@
         ],
         compiler_params=pltpu.CompilerParams(collective_id=0, has_side_effects=True),
     )(split_feature, split_bin, gradients, hessians, bin_words, children)
+    together = pltpu.with_memory_space_constraint(together, pltpu.VMEM)
     return pl.pallas_call(
         spread,
         out_shape=(

time: 44 us -> 42.6 us (0.968)
  Pallas kernels: 43.1 us -> 41.8 us
    pallas_call x1, Pallas kernels: 1.37 us -> 0.67 us  [on_device(): pl.pallas_call(spread, out_shape=(jax.ShapeDtypeStruct((2, BINS), F32), j...]
    pallas_call x1, Pallas kernels: 41.7 us -> 41.1 us  [on_device(): pl.pallas_call(kernel, out_shape=pltpu.VMEM((16, 128), F32), in_specs=[pl...]
where the time goes in v5:
time: 42.6 us; the launch traced here: 42.5 us
  Pallas kernels  41.8 us (98%)
  between operations  0.64 us (2%)
    pallas_call x1, Pallas kernels, on_device(): pl.pallas_call(kernel, out_shape=pltpu.VMEM((16, 128), F32), in_specs=[pl...  41.1 us

profile of v5, /device:TPU:1, one launch (start us, length us, event | category | flops | bytes accessed | tf_op | source)
XLA Modules:
  0.0 42.5 jit_solution(12328661659009194823)
XLA Ops:
  0.6 41.1 %shard_map.93.all_ref = f32[16,128]{1,0:T(8,128)S(1)} custom-call(s32[14]{0:T(128)} %split_feature_any.1, s32[14]{0:T(128)} %split_bin_any.1, bf16[512,128]{1,0:T(8,128)(2,1)} %grad_any.1, bf16[512]{0:T(512)(128)(2,1)} %hess_any.1, s32[32,512]{1,0:T(8,128)} %word_any.1, s32[3,512]{1,0:T(4,128)} %child_any.1), custom_call_target="tpu_custom_call" | custom-call | tf_op jit(solution)/shard_map/pallas_call | solution.py:456
  41.8 0.7 %shard_map.94 = (f32[2,64]{1,0:T(2,128)}, f32[4,64]{1,0:T(4,128)}, f32[8,64]{1,0:T(8,128)}, f32[3,1,2,128]{3,2,1,0:T(2,128)}) custom-call(f32[16,128]{1,0:T(8,128)S(1)} %shard_map.93.all_ref), custom_call_target="tpu_custom_call" | custom-call | tf_op jit(solution)/shard_map/pallas_call | solution.py:501

commit v6 on v5

--- a/solution.py
+++ b/solution.py
@@ -252,9 +252,8 @@
     bins = lax.broadcasted_iota(jnp.int32, (BINS, 1), 0).astype(F32)
 
     def add_rows(offset, first=False, after=None, places=range(NZ)):
-        here_x = pl.ds(places[0], len(places))
-        late = int(places[0] > 0)
-        arrived(got_x.at[offset, here_x], x_recv.at[offset, late])
+        for late in range(places[0] // 4, places[-1] // 4 + 1):
+            arrived(got_x.at[offset, pl.ds(4 * late, 4)], x_recv.at[offset, late])
         if offset == 0:
             pieces = [piece(i) for i in places]
             start = pl.multiple_of(HALF + 16 * block, 16)
@@ -262,7 +261,7 @@
             codes = [ref[pl.ds(start, 16), :] for ref in pieces]
             weights = [got_h[i] for i in places]
         else:
-            if not late:
+            if places[0] == 0:
                 arrived(got_yh.at[offset - 1], yh_recv.at[offset - 1])
             kept = [got_y[offset - 1, i, 0:HALF, :] for i in places]
             codes = [got_y[offset - 1, i, HALF:GOES_Y, :] for i in places]
@@ -326,26 +325,23 @@
         ).start()
         left_with(mine_z, pz_send.at[step])
     pltpu.make_async_copy(mine_z, part_z.at[z], pz_recv.at[z]).start()
+    add_rows(0, first=True, places=range(0, 8))
     from_y(1, 0)
     from_y(1, 1)
-    add_rows(0, first=True, places=range(NZ // 2))
-    add_rows(1, places=range(NZ // 2))
+    from_y(1, 2)
+    from_y(1, 3)
+    add_rows(1, places=range(0, 8))
     from_y(3, 0)
     from_y(3, 1)
-    add_rows(3, places=range(NZ // 2))
+    from_y(3, 2)
+    from_y(3, 3)
+    add_rows(3, places=range(0, 8))
     from_y(2, 0)
     from_y(2, 1)
-    add_rows(2, places=range(NZ // 2))
-    add_rows(0, places=range(NZ // 2, NZ))
-    from_y(1, 2)
-    from_y(1, 3)
-    add_rows(1, places=range(NZ // 2, NZ))
-    from_y(3, 2)
-    from_y(3, 3)
-    add_rows(3, places=range(NZ // 2, NZ))
+    add_rows(2, places=range(0, 4))
     from_y(2, 2)
     from_y(2, 3)
-    add_rows(2, places=range(NZ // 2, NZ), after=to_buddy)
+    add_rows(2, places=range(4, 8), after=to_buddy)
     for step in range(1, NY):
         left_with(got_y.at[0], y_send.at[step])
     for side in range(2):

time: 42.6 us -> 41.8 us (0.981)
  Pallas kernels: 41.8 us -> 41 us
    pallas_call x1, Pallas kernels: 41.1 us -> 40.3 us  [on_device(): pl.pallas_call(kernel, out_shape=pltpu.VMEM((16, 128), F32), in_specs=[pl...]
where the time goes in v6:
time: 41.8 us; the launch traced here: 41.6 us
  Pallas kernels  41 us (98%)
  between operations  0.64 us (2%)
    pallas_call x1, Pallas kernels, on_device(): pl.pallas_call(kernel, out_shape=pltpu.VMEM((16, 128), F32), in_specs=[pl...  40.3 us

profile of v6, /device:TPU:1, one launch (start us, length us, event | category | flops | bytes accessed | tf_op | source)
XLA Modules:
  0.0 41.6 jit_solution(15489449016652694100)
XLA Ops:
  0.6 40.3 %shard_map.93.all_ref = f32[16,128]{1,0:T(8,128)S(1)} custom-call(s32[14]{0:T(128)} %split_feature_any.1, s32[14]{0:T(128)} %split_bin_any.1, bf16[512,128]{1,0:T(8,128)(2,1)} %grad_any.1, bf16[512]{0:T(512)(128)(2,1)} %hess_any.1, s32[32,512]{1,0:T(8,128)} %word_any.1, s32[3,512]{1,0:T(4,128)} %child_any.1), custom_call_target="tpu_custom_call" | custom-call | tf_op jit(solution)/shard_map/pallas_call | solution.py:452
  41.0 0.7 %shard_map.94 = (f32[2,64]{1,0:T(2,128)}, f32[4,64]{1,0:T(4,128)}, f32[8,64]{1,0:T(8,128)}, f32[3,1,2,128]{3,2,1,0:T(2,128)}) custom-call(f32[16,128]{1,0:T(8,128)S(1)} %shard_map.93.all_ref), custom_call_target="tpu_custom_call" | custom-call | tf_op jit(solution)/shard_map/pallas_call | solution.py:497

commit v7 on v6

--- a/solution.py
+++ b/solution.py
@@ -241,7 +241,7 @@
                     here.at[pl.ds(start, 16)], got_y.at[NY - step - 1, place, pl.ds(HALF, 16)],
                     y_send.at[step], y_recv.at[NY - step - 1, group], at(y_to, z, core),
                 ).start()
-            for step in (0, 1, 3, 2) if group in DIRECT else (0,):
+            for step in (2, 1, 3, 0) if group in DIRECT else (0,):
                 to_x(here.at[pl.ds(0, HALF)], (NY - step) % NY, place, step)
 
     def from_y(offset, group):

time: 41.8 us -> 41.3 us (0.988)
  Pallas kernels: 41 us -> 40.5 us
    pallas_call x1, Pallas kernels: 40.3 us -> 39.9 us  [on_device(): pl.pallas_call(kernel, out_shape=pltpu.VMEM((16, 128), F32), in_specs=[pl...]
where the time goes in v7:
time: 41.3 us; the launch traced here: 41.2 us
  Pallas kernels  40.5 us (98%)
  between operations  0.64 us (2%)
    pallas_call x1, Pallas kernels, on_device(): pl.pallas_call(kernel, out_shape=pltpu.VMEM((16, 128), F32), in_specs=[pl...  39.9 us

profile of v7, /device:TPU:1, one launch (start us, length us, event | category | flops | bytes accessed | tf_op | source)
XLA Modules:
  0.0 41.2 jit_solution(5114201311846727173)
XLA Ops:
  0.6 39.9 %shard_map.93.all_ref = f32[16,128]{1,0:T(8,128)S(1)} custom-call(s32[14]{0:T(128)} %split_feature_any.1, s32[14]{0:T(128)} %split_bin_any.1, bf16[512,128]{1,0:T(8,128)(2,1)} %grad_any.1, bf16[512]{0:T(512)(128)(2,1)} %hess_any.1, s32[32,512]{1,0:T(8,128)} %word_any.1, s32[3,512]{1,0:T(4,128)} %child_any.1), custom_call_target="tpu_custom_call" | custom-call | tf_op jit(solution)/shard_map/pallas_call | solution.py:452
  40.5 0.7 %shard_map.94 = (f32[2,64]{1,0:T(2,128)}, f32[4,64]{1,0:T(4,128)}, f32[8,64]{1,0:T(8,128)}, f32[3,1,2,128]{3,2,1,0:T(2,128)}) custom-call(f32[16,128]{1,0:T(8,128)S(1)} %shard_map.93.all_ref), custom_call_target="tpu_custom_call" | custom-call | tf_op jit(solution)/shard_map/pallas_call | solution.py:497
